TPU v7x, 512 devices: a whole 4x4x16 slice. The times are simulated.
512 devices in a mesh: half: 4 (over x_hi, core), wide: 128 (over z, y, x_lo).
Axes of the slice: x: 4 (x_hi: 2, x_lo: 2; x = x_hi * 2 + x_lo), y: 4, z: 16, core: 2. Of those that a mesh axis runs over, the one named last changes fastest.
Arguments:
- gains: float32 [4096, 4096], P(('half', 'wide')), parts along dimension 0, may hold values from -4 to 4
- response: bfloat16 [4096, 4096], P('wide', 'half'), parts along dimension 1, may hold values from -6 to 6
- student: bfloat16 [4096, 4096], P('wide', 'half'), parts along dimension 1, may hold values from 0.19921875 to 1
- blocks: bfloat16 [16, 256, 256], P('half'), parts along dimension 0, may hold values from -0.5 to 2.5, as said below
- order: int32 [4096], P('half'), parts along dimension 0, may hold values from 0 to 1023, each once
- lower: float32 [4096], P(('half', 'wide')), parts along dimension 0, may hold values from -1.2 to -0.4
- upper: float32 [4096], P(('half', 'wide')), parts along dimension 0, may hold values from 0.4 to 1.2
- lengths: float32 [4096], replicated, may hold values from 32 to 2048
- amplitude: float32 [4096], replicated, may hold values from 0.5 to 1.5
Outputs:
- tracked: float32 [4096, 4096], P(('half', 'wide')), parts along dimension 0
There are 4 independent parts, one for each index of `half`. A program takes and returns all parts, laid end to end along the dimension named above; an argument that names none is the same for every part. Nothing has to cross between parts.
Inputs may be any that keep to these rules, and one draw needn't show every extreme that they name: `blocks`: each block is symmetric.
All inputs are finite; a program needn't handle non-finite values.
Results may differ from a plain program's by a relative error of at most 0.012.
The roundings to bfloat16 on the way count: a program that leaves them out, or rounds other values in their place, can miss the bound.
Values may be sent and summed in bfloat16 or wider, within the bound.
A program may use at most 128 MiB of HBM per device.

v0:
```python
import jax
import jax.numpy as jnp
from jax import lax
from jax.sharding import PartitionSpec as P

ITERS = 2


def covar_stack(lengths, amplitude, span):
    total = lengths.shape[0]
    count = total // span
    rows = jnp.arange(total, dtype=jnp.int32)

    def one_block(index):
        start = index * span
        cols = start + jnp.arange(span, dtype=jnp.int32)
        diff = (rows[:, None] - cols[None, :]).astype(lengths.dtype)
        left = lengths[:, None]
        right = lax.dynamic_slice_in_dim(lengths, start, span, 0)[None, :]
        amp_right = lax.dynamic_slice_in_dim(amplitude, start, span, 0)[None, :]
        denom = left * left + right * right
        vals = (
            amplitude[:, None]
            * amp_right
            * jnp.sqrt(2.0 * left * right / denom)
            * jnp.exp(-diff * diff / denom)
        )
        return vals.astype(jnp.bfloat16)

    return lax.map(one_block, jnp.arange(count, dtype=jnp.int32))


def data_rows(packed, resp_perm, stud_perm, blocks, order, inverse):
    rows, chans = packed.shape
    nblk, width = (blocks.shape[0], blocks.shape[1])
    moved = jnp.take(packed, order, axis=1).reshape(rows, nblk, width)
    product = jnp.einsum("rbi,bij->rbj", moved, blocks, preferred_element_type=jnp.float32).reshape(
        rows, chans
    )
    permuted = stud_perm.astype(jnp.float32) * (product - resp_perm.astype(jnp.float32))
    return jnp.take(permuted, inverse, axis=1).astype(jnp.bfloat16)


def per_device(gains, response, student, blocks, order, lower, upper, lengths, amplitude):
    nwide = lax.axis_size("wide")
    chd, epochs = gains.shape
    epd = epochs // nwide
    chans = chd * nwide
    inverse = jnp.zeros((chans,), jnp.int32).at[order].set(jnp.arange(chans, dtype=jnp.int32))
    resp_perm = jnp.take(response, order, axis=1)
    stud_perm = jnp.take(student, order, axis=1)
    span = min(256, epochs)
    kernel_stack = covar_stack(lengths, amplitude, span)
    current = gains
    for step in range(ITERS):
        packed = current.astype(jnp.bfloat16).reshape(chd, nwide, epd)
        got = (
            lax.all_to_all(packed, "wide", split_axis=1, concat_axis=0, tiled=True)
            .reshape(chans, epd)
            .T
        )
        misfit_rows = data_rows(got, resp_perm, stud_perm, blocks, order, inverse)
        misfit = lax.all_to_all(
            misfit_rows.T.reshape(chans, 1, epd), "wide", split_axis=0, concat_axis=1, tiled=True
        ).reshape(chd, epochs)
        smoothed = jnp.einsum(
            "ce,bes->cbs", misfit, kernel_stack, preferred_element_type=jnp.float32
        ).reshape(chd, epochs)
        current = jnp.clip(current - 0.02 * smoothed, lower[:, None], upper[:, None])
    return current


def solution(mesh):
    placed = (
        P(("half", "wide"), None),
        P("wide", "half"),
        P("wide", "half"),
        P("half", None, None),
        P("half"),
        P(("half", "wide")),
        P(("half", "wide")),
        P(),
        P(),
    )
    return jax.shard_map(
        per_device, mesh=mesh, in_specs=placed, out_specs=P(("half", "wide"), None), check_vma=False
    )
```

profile of v0, /device:TPU:4, one launch (start us, length us, event | category | flops | bytes accessed | tf_op | source)
XLA Modules:
  0.0 323.4 jit_solution(1157350678906811121)
XLA Ops:
  2.2 20.6 %all-to-all-start = ((bf16[128,2,128]{2,1,0:T(2,128)(2,1)}), bf16[128,2,128]{2,1,0:T(2,128)(2,1)S(1)}, u32[]{:S(2)}, u32[]{:S(2)}) async-start(bf16[128,2,128]{2,1,0:T(2,128)(2,1)} %reshape.377), calls=%async_computation | async-start | bytes 131072 | tf_op jit(solution)/shard_map/all_to_all | solution.py:58
  24.1 4.3 %scatter_custom_fusion = s32[1024]{0:T(1024)S(1)} fusion(s32[1024]{0:T(1024)S(1)} %get-tuple-element.97, s32[1024]{0:T(1024)S(1)} %iota.15, s32[]{:T(128)} %constant.36.clone.1), kind=kCustom, calls=%fused_computation.51 | custom fusion | bytes 4100 | tf_op jit(solution)/shard_map/scatter | solution.py:49
  29.5 3.2 gather_fusion
  33.9 3.2 gather_fusion.2
  38.2 3.2 gather_fusion.1
  42.1 3.2 gather_fusion.3
  47.8 17.2 %all-to-all-start.1 = ((bf16[128,2,128]{2,1,0:T(2,128)(2,1)}), bf16[128,2,128]{2,1,0:T(2,128)(2,1)S(1)}, u32[]{:S(2)}, u32[]{:S(2)}) async-start(bf16[128,2,128]{2,1,0:T(2,128)(2,1)} %reshape.379), calls=%async_computation.1 | async-start | bytes 131072 | tf_op jit(solution)/shard_map/all_to_all | solution.py:63
  65.1 166.4 %while.12 = (s32[]{:T(128)}, bf16[16,4096,256]{1,2,0:T(8,128)(2,1)}, f32[4096]{0:T(1024)S(1)}, s32[16]{0:T(128)S(1)}, f32[4096]{0:T(1024)S(1)}, /*index=5*/f32[4...) while((s32[]{:T(128)}, bf16[16,4096,256]{1,2,0:T(8,128)(2,1)}, ...), condition=%wide.region_2.5_spmd.clone, body=%wide.region_1.4_spmd.clone.sunk | while | flops 12587526 | bytes 10578603 | solution.py:30
  66.5 4.6 %fusion.32 = bf16[1,4096,256]{2,1,0:T(8,128)(2,1)} fusion(s32[256]{0:T(256)S(1)} %iota_add_fusion.2, f32[256]{0:T(256)S(1)} %get-tuple-element.140, f32[4096]{0:T(1024)S(1)} %bitcast.109, f32[256]{0:T(256)S(1)} %get-tuple-element.141, f32[4096]{0:T(1024)S(1)} %broadcast_multiply_fusion.2, f32[256]{0:T(256)S(1)} %dynamic_slice.22, ...), kind=kLoop, calls=%fused_computation.17.clone.1 | loop fusion | flops 12582912 | bytes 2150400 | tf_op jit(solution)/shard_map/while/body/eval_jaxpr/convert_element_type | solution.py:28
  71.1 2.9 copy.95
  76.9 4.6 %fusion.32 = bf16[1,4096,256]{2,1,0:T(8,128)(2,1)} fusion(s32[256]{0:T(256)S(1)} %iota_add_fusion.2, f32[256]{0:T(256)S(1)} %get-tuple-element.140, f32[4096]{0:T(1024)S(1)} %bitcast.109, f32[256]{0:T(256)S(1)} %get-tuple-element.141, f32[4096]{0:T(1024)S(1)} %broadcast_multiply_fusion.2, f32[256]{0:T(256)S(1)} %dynamic_slice.22, ...), kind=kLoop, calls=%fused_computation.17.clone.1 | loop fusion | flops 12582912 | bytes 2150400 | tf_op jit(solution)/shard_map/while/body/eval_jaxpr/convert_element_type | solution.py:28
  81.5 2.9 copy.95
  87.3 4.6 %fusion.32 = bf16[1,4096,256]{2,1,0:T(8,128)(2,1)} fusion(s32[256]{0:T(256)S(1)} %iota_add_fusion.2, f32[256]{0:T(256)S(1)} %get-tuple-element.140, f32[4096]{0:T(1024)S(1)} %bitcast.109, f32[256]{0:T(256)S(1)} %get-tuple-element.141, f32[4096]{0:T(1024)S(1)} %broadcast_multiply_fusion.2, f32[256]{0:T(256)S(1)} %dynamic_slice.22, ...), kind=kLoop, calls=%fused_computation.17.clone.1 | loop fusion | flops 12582912 | bytes 2150400 | tf_op jit(solution)/shard_map/while/body/eval_jaxpr/convert_element_type | solution.py:28
  91.9 2.9 copy.95
  97.7 4.6 %fusion.32 = bf16[1,4096,256]{2,1,0:T(8,128)(2,1)} fusion(s32[256]{0:T(256)S(1)} %iota_add_fusion.2, f32[256]{0:T(256)S(1)} %get-tuple-element.140, f32[4096]{0:T(1024)S(1)} %bitcast.109, f32[256]{0:T(256)S(1)} %get-tuple-element.141, f32[4096]{0:T(1024)S(1)} %broadcast_multiply_fusion.2, f32[256]{0:T(256)S(1)} %dynamic_slice.22, ...), kind=kLoop, calls=%fused_computation.17.clone.1 | loop fusion | flops 12582912 | bytes 2150400 | tf_op jit(solution)/shard_map/while/body/eval_jaxpr/convert_element_type | solution.py:28
  102.3 2.9 copy.95
  108.1 4.6 %fusion.32 = bf16[1,4096,256]{2,1,0:T(8,128)(2,1)} fusion(s32[256]{0:T(256)S(1)} %iota_add_fusion.2, f32[256]{0:T(256)S(1)} %get-tuple-element.140, f32[4096]{0:T(1024)S(1)} %bitcast.109, f32[256]{0:T(256)S(1)} %get-tuple-element.141, f32[4096]{0:T(1024)S(1)} %broadcast_multiply_fusion.2, f32[256]{0:T(256)S(1)} %dynamic_slice.22, ...), kind=kLoop, calls=%fused_computation.17.clone.1 | loop fusion | flops 12582912 | bytes 2150400 | tf_op jit(solution)/shard_map/while/body/eval_jaxpr/convert_element_type | solution.py:28
  112.7 2.9 copy.95
  115.6 1.5 constant_dynamic-update-slice_fusion.2
  118.5 4.6 %fusion.32 = bf16[1,4096,256]{2,1,0:T(8,128)(2,1)} fusion(s32[256]{0:T(256)S(1)} %iota_add_fusion.2, f32[256]{0:T(256)S(1)} %get-tuple-element.140, f32[4096]{0:T(1024)S(1)} %bitcast.109, f32[256]{0:T(256)S(1)} %get-tuple-element.141, f32[4096]{0:T(1024)S(1)} %broadcast_multiply_fusion.2, f32[256]{0:T(256)S(1)} %dynamic_slice.22, ...), kind=kLoop, calls=%fused_computation.17.clone.1 | loop fusion | flops 12582912 | bytes 2150400 | tf_op jit(solution)/shard_map/while/body/eval_jaxpr/convert_element_type | solution.py:28
  123.1 2.9 copy.95
  128.9 4.6 %fusion.32 = bf16[1,4096,256]{2,1,0:T(8,128)(2,1)} fusion(s32[256]{0:T(256)S(1)} %iota_add_fusion.2, f32[256]{0:T(256)S(1)} %get-tuple-element.140, f32[4096]{0:T(1024)S(1)} %bitcast.109, f32[256]{0:T(256)S(1)} %get-tuple-element.141, f32[4096]{0:T(1024)S(1)} %broadcast_multiply_fusion.2, f32[256]{0:T(256)S(1)} %dynamic_slice.22, ...), kind=kLoop, calls=%fused_computation.17.clone.1 | loop fusion | flops 12582912 | bytes 2150400 | tf_op jit(solution)/shard_map/while/body/eval_jaxpr/convert_element_type | solution.py:28
  133.5 2.9 copy.95
  139.3 4.6 %fusion.32 = bf16[1,4096,256]{2,1,0:T(8,128)(2,1)} fusion(s32[256]{0:T(256)S(1)} %iota_add_fusion.2, f32[256]{0:T(256)S(1)} %get-tuple-element.140, f32[4096]{0:T(1024)S(1)} %bitcast.109, f32[256]{0:T(256)S(1)} %get-tuple-element.141, f32[4096]{0:T(1024)S(1)} %broadcast_multiply_fusion.2, f32[256]{0:T(256)S(1)} %dynamic_slice.22, ...), kind=kLoop, calls=%fused_computation.17.clone.1 | loop fusion | flops 12582912 | bytes 2150400 | tf_op jit(solution)/shard_map/while/body/eval_jaxpr/convert_element_type | solution.py:28
  143.9 2.9 copy.95
  149.7 4.6 %fusion.32 = bf16[1,4096,256]{2,1,0:T(8,128)(2,1)} fusion(s32[256]{0:T(256)S(1)} %iota_add_fusion.2, f32[256]{0:T(256)S(1)} %get-tuple-element.140, f32[4096]{0:T(1024)S(1)} %bitcast.109, f32[256]{0:T(256)S(1)} %get-tuple-element.141, f32[4096]{0:T(1024)S(1)} %broadcast_multiply_fusion.2, f32[256]{0:T(256)S(1)} %dynamic_slice.22, ...), kind=kLoop, calls=%fused_computation.17.clone.1 | loop fusion | flops 12582912 | bytes 2150400 | tf_op jit(solution)/shard_map/while/body/eval_jaxpr/convert_element_type | solution.py:28
  154.3 2.9 copy.95
  160.1 4.6 %fusion.32 = bf16[1,4096,256]{2,1,0:T(8,128)(2,1)} fusion(s32[256]{0:T(256)S(1)} %iota_add_fusion.2, f32[256]{0:T(256)S(1)} %get-tuple-element.140, f32[4096]{0:T(1024)S(1)} %bitcast.109, f32[256]{0:T(256)S(1)} %get-tuple-element.141, f32[4096]{0:T(1024)S(1)} %broadcast_multiply_fusion.2, f32[256]{0:T(256)S(1)} %dynamic_slice.22, ...), kind=kLoop, calls=%fused_computation.17.clone.1 | loop fusion | flops 12582912 | bytes 2150400 | tf_op jit(solution)/shard_map/while/body/eval_jaxpr/convert_element_type | solution.py:28
  164.7 2.9 copy.95
  170.5 4.6 %fusion.32 = bf16[1,4096,256]{2,1,0:T(8,128)(2,1)} fusion(s32[256]{0:T(256)S(1)} %iota_add_fusion.2, f32[256]{0:T(256)S(1)} %get-tuple-element.140, f32[4096]{0:T(1024)S(1)} %bitcast.109, f32[256]{0:T(256)S(1)} %get-tuple-element.141, f32[4096]{0:T(1024)S(1)} %broadcast_multiply_fusion.2, f32[256]{0:T(256)S(1)} %dynamic_slice.22, ...), kind=kLoop, calls=%fused_computation.17.clone.1 | loop fusion | flops 12582912 | bytes 2150400 | tf_op jit(solution)/shard_map/while/body/eval_jaxpr/convert_element_type | solution.py:28
  175.1 2.9 copy.95
  180.8 4.6 %fusion.32 = bf16[1,4096,256]{2,1,0:T(8,128)(2,1)} fusion(s32[256]{0:T(256)S(1)} %iota_add_fusion.2, f32[256]{0:T(256)S(1)} %get-tuple-element.140, f32[4096]{0:T(1024)S(1)} %bitcast.109, f32[256]{0:T(256)S(1)} %get-tuple-element.141, f32[4096]{0:T(1024)S(1)} %broadcast_multiply_fusion.2, f32[256]{0:T(256)S(1)} %dynamic_slice.22, ...), kind=kLoop, calls=%fused_computation.17.clone.1 | loop fusion | flops 12582912 | bytes 2150400 | tf_op jit(solution)/shard_map/while/body/eval_jaxpr/convert_element_type | solution.py:28
  185.5 2.9 copy.95
  191.2 4.6 %fusion.32 = bf16[1,4096,256]{2,1,0:T(8,128)(2,1)} fusion(s32[256]{0:T(256)S(1)} %iota_add_fusion.2, f32[256]{0:T(256)S(1)} %get-tuple-element.140, f32[4096]{0:T(1024)S(1)} %bitcast.109, f32[256]{0:T(256)S(1)} %get-tuple-element.141, f32[4096]{0:T(1024)S(1)} %broadcast_multiply_fusion.2, f32[256]{0:T(256)S(1)} %dynamic_slice.22, ...), kind=kLoop, calls=%fused_computation.17.clone.1 | loop fusion | flops 12582912 | bytes 2150400 | tf_op jit(solution)/shard_map/while/body/eval_jaxpr/convert_element_type | solution.py:28
  195.9 2.9 copy.95
  198.8 1.5 constant_dynamic-update-slice_fusion.2
  201.7 4.6 %fusion.32 = bf16[1,4096,256]{2,1,0:T(8,128)(2,1)} fusion(s32[256]{0:T(256)S(1)} %iota_add_fusion.2, f32[256]{0:T(256)S(1)} %get-tuple-element.140, f32[4096]{0:T(1024)S(1)} %bitcast.109, f32[256]{0:T(256)S(1)} %get-tuple-element.141, f32[4096]{0:T(1024)S(1)} %broadcast_multiply_fusion.2, f32[256]{0:T(256)S(1)} %dynamic_slice.22, ...), kind=kLoop, calls=%fused_computation.17.clone.1 | loop fusion | flops 12582912 | bytes 2150400 | tf_op jit(solution)/shard_map/while/body/eval_jaxpr/convert_element_type | solution.py:28
  206.3 2.9 copy.95
  212.1 4.6 %fusion.32 = bf16[1,4096,256]{2,1,0:T(8,128)(2,1)} fusion(s32[256]{0:T(256)S(1)} %iota_add_fusion.2, f32[256]{0:T(256)S(1)} %get-tuple-element.140, f32[4096]{0:T(1024)S(1)} %bitcast.109, f32[256]{0:T(256)S(1)} %get-tuple-element.141, f32[4096]{0:T(1024)S(1)} %broadcast_multiply_fusion.2, f32[256]{0:T(256)S(1)} %dynamic_slice.22, ...), kind=kLoop, calls=%fused_computation.17.clone.1 | loop fusion | flops 12582912 | bytes 2150400 | tf_op jit(solution)/shard_map/while/body/eval_jaxpr/convert_element_type | solution.py:28
  216.7 2.9 copy.95
  222.5 4.6 %fusion.32 = bf16[1,4096,256]{2,1,0:T(8,128)(2,1)} fusion(s32[256]{0:T(256)S(1)} %iota_add_fusion.2, f32[256]{0:T(256)S(1)} %get-tuple-element.140, f32[4096]{0:T(1024)S(1)} %bitcast.109, f32[256]{0:T(256)S(1)} %get-tuple-element.141, f32[4096]{0:T(1024)S(1)} %broadcast_multiply_fusion.2, f32[256]{0:T(256)S(1)} %dynamic_slice.22, ...), kind=kLoop, calls=%fused_computation.17.clone.1 | loop fusion | flops 12582912 | bytes 2150400 | tf_op jit(solution)/shard_map/while/body/eval_jaxpr/convert_element_type | solution.py:28
  227.1 2.9 copy.95
  232.2 14.5 %fusion.20 = (bf16[8,4096]{1,0:T(8,128)(2,1)S(1)}, f32[8,4096]{1,0:T(8,128)S(1)}) fusion(f32[8,4096]{1,0:T(8,128)S(1)} %copy-done.2, bf16[8,4096]{1,0:T(8,128)(2,1)S(1)} %reshape.293, bf16[4096,4096]{1,0:T(8,128)(2,1)} %bitcast.98, f32[8]{0:T(128)S(1)} %copy-done.3, f32[8]{0:T(128)S(1)} %copy-done.4), kind=kOutput, calls=%fused_computation.54 | convolution fusion | flops 268599296 | bytes 33947712 | tf_op jit(solution)/shard_map/ce,bes->cbs/dot_general | solution.py:66
  247.2 31.4 %all_to_all.60 = bf16[128,2,128]{2,1,0:T(2,128)(2,1)S(1)} all-to-all(bf16[128,2,128]{2,1,0:T(2,128)(2,1)S(1)} %reshape.381), channel_id=1, replica_groups=mesh['half'=4,'wide'=128] {'wide'}, dimensions={0} | all-to-all | bytes 131072 | tf_op jit(solution)/shard_map/all_to_all | solution.py:58
  278.8 3.2 gather_fusion.4
  282.7 3.2 gather_fusion.5
  287.2 20.4 %all_to_all.61 = bf16[128,2,128]{2,1,0:T(2,128)(2,1)S(1)} all-to-all(bf16[128,2,128]{2,1,0:T(2,128)(2,1)S(1)} %reshape.383), channel_id=1, replica_groups=mesh['half'=4,'wide'=128] {'wide'}, dimensions={0} | all-to-all | bytes 131072 | tf_op jit(solution)/shard_map/all_to_all | solution.py:63
  308.2 15.2 %fusion.13 = f32[8,4096]{1,0:T(8,128)} fusion(f32[8,4096]{1,0:T(8,128)S(1)} %get-tuple-element.100, bf16[8,4096]{1,0:T(8,128)(2,1)S(1)} %reshape.299, bf16[4096,4096]{1,0:T(8,128)(2,1)} %bitcast.99, f32[8]{0:T(128)S(1)} %copy-done.3, f32[8]{0:T(128)S(1)} %copy-done.4), kind=kOutput, calls=%fused_computation.28 | convolution fusion | flops 268566528 | bytes 33882176 | tf_op jit(solution)/shard_map/ce,bes->cbs/dot_general | solution.py:66
  (156 shorter events, 46.4 us)
Async XLA Ops:
  0.0 41.6 %copy-start = (bf16[4,256,256]{2,1,0:T(8,128)(2,1)S(1)}, bf16[4,256,256]{2,1,0:T(8,128)(2,1)}, u32[]{:S(2)}) copy-start(bf16[4,256,256]{2,1,0:T(8,128)(2,1)} %param.18) | copy-start | bytes 1572868
  2.2 35.9 %all-to-all-start = ((bf16[128,2,128]{2,1,0:T(2,128)(2,1)}), bf16[128,2,128]{2,1,0:T(2,128)(2,1)S(1)}, u32[]{:S(2)}, u32[]{:S(2)}) async-start(bf16[128,2,128]{2,1,0:T(2,128)(2,1)} %reshape.377), calls=%async_computation | async-start | bytes 131072 | tf_op jit(solution)/shard_map/all_to_all | solution.py:58
  28.5 36.5 %copy-start.1 = (f32[4096]{0:T(1024)S(1)}, f32[4096]{0:T(1024)}, u32[]{:S(2)}) copy-start(f32[4096]{0:T(1024)} %param.22) | copy-start | bytes 49156
  28.5 36.5 %copy-start.5 = (f32[4096]{0:T(1024)S(1)}, f32[4096]{0:T(1024)}, u32[]{:S(2)}) copy-start(f32[4096]{0:T(1024)} %param.23) | copy-start | bytes 49156
  47.8 183.6 %all-to-all-start.1 = ((bf16[128,2,128]{2,1,0:T(2,128)(2,1)}), bf16[128,2,128]{2,1,0:T(2,128)(2,1)S(1)}, u32[]{:S(2)}, u32[]{:S(2)}) async-start(bf16[128,2,128]{2,1,0:T(2,128)(2,1)} %reshape.379), calls=%async_computation.1 | async-start | bytes 131072 | tf_op jit(solution)/shard_map/all_to_all | solution.py:63
  65.0 167.1 %copy-start.2 = (f32[8,4096]{1,0:T(8,128)S(1)}, f32[8,4096]{1,0:T(8,128)}, u32[]{:S(2)}) copy-start(f32[8,4096]{1,0:T(8,128)} %param.15) | copy-start | bytes 393220
  65.1 167.1 %copy-start.3 = (f32[8]{0:T(128)S(1)}, f32[8]{0:T(128)}, u32[]{:S(2)}) copy-start(f32[8]{0:T(128)} %param.20) | copy-start | bytes 100
  65.1 167.1 %copy-start.4 = (f32[8]{0:T(128)S(1)}, f32[8]{0:T(128)}, u32[]{:S(2)}) copy-start(f32[8]{0:T(128)} %param.21) | copy-start | bytes 100
where the time goes:
time: 325 us; the launch traced here: 323 us
  local copies, waits for them, and re-layouts  112 us (34%)
  other arithmetic  81.2 us (25%)
  blocking collectives  51.8 us (16%)
  starting transfers between devices  37.8 us (12%)
  matrix products  30.1 us (9%)
  loops' own time  10.2 us (3%)
    convert_element_type x16, other arithmetic, one_block(): return vals.astype(jnp.bfloat16)  74 us
    dynamic_update_slice x32, local copies, waits for them, and re-layouts, covar_stack(): return lax.map(one_block, jnp.arange(count, dtype=jnp.int32))  70.1 us
    all_to_all x1, blocking collectives, per_device(): lax.all_to_all(packed, 'wide', split_axis=1, concat_axis=0, tiled=True)  31.4 us
    dot_general x2, matrix products, per_device(): jnp.einsum('ce,bes->cbs', misfit, kernel_stack, preferred_element_type=jn...  29.6 us
    all_to_all x1, starting transfers between devices, per_device(): lax.all_to_all(packed, 'wide', split_axis=1, concat_axis=0, tiled=True)  20.6 us
    all_to_all x1, blocking collectives, per_device(): lax.all_to_all(misfit_rows.T.reshape(chans, 1, epd), 'wide', split_axis=0...  20.4 us
    all_to_all x1, starting transfers between devices, per_device(): lax.all_to_all(misfit_rows.T.reshape(chans, 1, epd), 'wide', split_axis=0...  17.2 us
    another operation x1, loops' own time, covar_stack(): return lax.map(one_block, jnp.arange(count, dtype=jnp.int32))  10.2 us
  transfers between devices with their start and end apart: 2, of which 0 were waited for; matrix products, arithmetic and copies ran while one was open for 53% of the time, Pallas kernels for 0%

commit v1 on v0

v1 whole, which is shorter than its diff:
```python
import functools

import jax
import jax.numpy as jnp
from jax import lax
from jax.experimental import pallas as pl
from jax.experimental.pallas import tpu as pltpu
from jax.sharding import PartitionSpec as P

ITERS = 2
F32 = jnp.float32
BF16 = jnp.bfloat16
NT = (((1,), (1,)), ((), ()))


def swap_blocks(parts, quarter):
    out = []
    for b in range(4):
        acc = None
        for g in range(4):
            moved = parts[g] if g == b else pltpu.roll(parts[g], (32 * (g - b)) % 128, 1)
            acc = moved if acc is None else jnp.where(quarter == g, moved, acc)
        out.append(acc)
    return out


def kernel(
    gains, bounds, response, student, blocks, order, lengths, amplitude, out,
    start_send, start_recv, state, bound_lo, bound_hi,
    pack_send, pack_recv, mis_send, mis_recv, gathered, final_send, final_recv,
    onehot, matrix, resp_tile, stud_tile, spread, covar, len_row, amp_row, len_col, amp_col, dist,
    plane_send_sem, plane_recv_sem, col_send_sem, col_recv_sem,
):
    wide = lax.axis_index("wide")
    z = wide // 8
    yx = wide % 8

    def at_plane(k):
        t = (yx + k) % 8
        return t, {"wide": z * 8 + t}

    def at_column(k):
        t = (z + k) % 16
        return t, {"wide": t * 8 + yx}

    barrier = pltpu.get_barrier_semaphore()
    for k in range(1, 16):
        _, dev = at_column(k)
        pl.semaphore_signal(barrier, inc=1, device_id=dev, device_id_type=pl.DeviceIdType.MESH)
    for k in range(1, 8):
        _, dev = at_plane(k)
        pl.semaphore_signal(barrier, inc=1, device_id=dev, device_id_type=pl.DeviceIdType.MESH)

    def remote(src, dst, ssem, rsem, dev):
        return pltpu.make_async_remote_copy(
            src_ref=src, dst_ref=dst, send_sem=ssem, recv_sem=rsem,
            device_id=dev, device_id_type=pl.DeviceIdType.MESH,
        )

    quarter8 = lax.broadcasted_iota(jnp.int32, (8, 128), 1) // 32
    quarter16 = lax.broadcasted_iota(jnp.int32, (16, 128), 1) // 32
    quarter256 = lax.broadcasted_iota(jnp.int32, (256, 128), 1) // 32

    for h in range(2):
        for a in range(4):
            parts = [gains[:, pl.ds(128 * (2 * (4 * a + b) + h), 128)] for b in range(4)]
            for c, y in enumerate(swap_blocks(parts, quarter8)):
                start_send[4 * h + c, :, pl.ds(128 * a, 128)] = y
    for t in range(8):
        start_send[t, :, pl.ds(512, 128)] = bounds[...]

    pl.semaphore_wait(barrier, 22)

    starts = []
    for k in range(1, 8):
        t, dev = at_plane(k)
        c = remote(start_send.at[t], start_recv.at[yx], plane_send_sem.at[0, k], plane_recv_sem.at[0, k], dev)
        c.start()
        starts.append(c)
    start_recv[yx] = start_send[yx]

    row = lax.broadcasted_iota(jnp.int32, (1024, 128), 0)
    chan = ((row // 16) % 16) * 64 + (row // 256) * 16 + row % 16
    for j in range(8):
        onehot[:, pl.ds(128 * j, 128)] = jnp.where(chan == order[pl.ds(j, 1), :], 1.0, 0.0).astype(BF16)

    @pl.loop(0, 4)
    def _(q):
        rows = pl.ds(pl.multiple_of(q * 256, 256), 256)
        for b in range(4):
            spread[:, pl.ds(256 * b, 256)] = jnp.dot(
                onehot[rows, pl.ds(256 * b, 256)], blocks[b], preferred_element_type=F32
            ).astype(BF16)
        matrix[rows, :] = lax.dot_general(
            spread[...], onehot[...], NT, preferred_element_type=F32
        ).astype(BF16)

    for c in starts:
        c.wait()
    for s in range(8):
        state[pl.ds(8 * s, 8), :] = start_recv[s, :, pl.ds(0, 512)]
        bound_lo[pl.ds(8 * s, 8), :] = jnp.broadcast_to(start_recv[s, :, pl.ds(512, 1)], (8, 128))
        bound_hi[pl.ds(8 * s, 8), :] = jnp.broadcast_to(start_recv[s, :, pl.ds(576, 1)], (8, 128))

    def send_column(it, which, send, recv):
        copies = []
        for k in (8, 7, 9, 6, 10, 5, 11, 4, 12, 3, 13, 2, 14, 1, 15):
            t, dev = at_column(k)
            c = remote(send.at[t], recv.at[it, z], col_send_sem.at[it, which, k], col_recv_sem.at[it, which, k], dev)
            c.start()
            copies.append(c)
        recv[it, z] = send[z]
        return copies

    def prepare_rest():
        for src, dst in ((response, resp_tile), (student, stud_tile)):
            x = src[...].astype(F32)
            tall = jnp.transpose(jnp.concatenate([x, x, x, x], axis=0))
            for t in range(16):
                acc = tall[64 * t : 64 * t + 16]
                for g in range(1, 4):
                    acc = jnp.where(quarter16 == g, tall[64 * t + 16 * g : 64 * t + 16 * g + 16], acc)
                dst[pl.ds(16 * t, 16), :] = acc

    def prepare_covar():
        quarter4 = lax.broadcasted_iota(jnp.int32, (4, 128), 1) // 32
        for src, dst in ((lengths, len_row), (amplitude, amp_row)):
            for h in range(2):
                parts = [
                    jnp.concatenate([src[pl.ds(h + 2 * b + 8 * a, 1), :] for a in range(4)], axis=0)
                    for b in range(4)
                ]
                for c, y in enumerate(swap_blocks(parts, quarter4)):
                    dst[4 * h + c, pl.ds(0, 4), :] = y
        own_len = len_row[yx]
        own_amp = amp_row[yx]
        for a in range(4):
            lc = jnp.transpose(jnp.broadcast_to(own_len[a : a + 1, :], (128, 128)))
            ac = jnp.transpose(jnp.broadcast_to(own_amp[a : a + 1, :], (128, 128)))
            len_col[a] = lc * lc
            amp_col[a] = ac * jnp.sqrt(2.0 * lc)
        i0 = lax.broadcasted_iota(jnp.int32, (128, 128), 0)
        i1 = lax.broadcasted_iota(jnp.int32, (128, 128), 1)
        dist[...] = ((i0 // 32 - i1 // 32) * 256 + i0 % 32 - i1 % 32).astype(F32)

        @pl.loop(0, 8)
        def _(t):
            lrow = len_row[t]
            arow = amp_row[t]
            for b in range(4):
                lr = lrow[b : b + 1, :]
                sq = lr * lr
                ar = arow[b : b + 1, :] * jnp.sqrt(lr)
                for a in range(4):
                    shift = ((a - b) * 1024 + (yx - t) * 32).astype(F32)
                    d = dist[...] + shift
                    inv = lax.rsqrt(len_col[a] + sq)
                    q = d * inv
                    vals = (amp_col[a] * ar) * (inv * jnp.exp(-(q * q)))
                    covar[pl.ds(128 * a, 128), pl.ds(pl.multiple_of(512 * t + 128 * b, 128), 128)] = vals.astype(BF16)

    for it in range(ITERS):
        for a in range(4):
            parts = [state[pl.ds(16 * g, 16), pl.ds(128 * a, 128)] for g in range(4)]
            for b, y in enumerate(swap_blocks(parts, quarter16)):
                pack_send[4 * a + b] = y.astype(BF16)
        copies = send_column(it, 0, pack_send, pack_recv)
        if it == 0:
            prepare_rest()
        for c in copies:
            c.wait()
        got = pack_recv[it].astype(F32).reshape(256, 128)
        for g in range(4):
            x = jnp.where(quarter256 == g, got, 0.0)
            x = x + pltpu.roll(x, 32, 1)
            x = x + pltpu.roll(x, 64, 1)
            spread[:, pl.ds(128 * g, 128)] = x.astype(BF16)
        prod = None
        for g2 in range(4):
            acc = None
            for g in range(4):
                p = jnp.dot(
                    matrix[pl.ds(256 * g2, 256), pl.ds(256 * g, 256)], spread[:, pl.ds(128 * g, 128)],
                    preferred_element_type=F32,
                )
                acc = p if acc is None else acc + p
            prod = acc if prod is None else jnp.where(quarter256 == g2, acc, prod)
        misfit = (stud_tile[...] * (prod - resp_tile[...])).astype(BF16)
        mis_send[...] = misfit.reshape(16, 16, 128)
        copies = send_column(it, 1, mis_send, mis_recv)
        if it == 0:
            prepare_covar()
        for c in copies:
            c.wait()
        for a in range(4):
            parts = [mis_recv[it, 4 * a + b].astype(F32) for b in range(4)]
            for g, y in enumerate(swap_blocks(parts, quarter16)):
                gathered[it, yx, pl.ds(16 * g, 16), pl.ds(128 * a, 128)] = y.astype(BF16)
        copies = []
        for k in range(1, 8):
            t, dev = at_plane(k)
            c = remote(
                gathered.at[it, yx], gathered.at[it, yx],
                plane_send_sem.at[1 + it, k], plane_recv_sem.at[1 + it, k], dev,
            )
            c.start()
            copies.append(c)
        smoothed = None
        for k in range(8):
            if k:
                copies[k - 1].wait_recv()
            t = (yx - k + 8) % 8
            p = lax.dot_general(
                gathered[it, t], covar[:, pl.ds(pl.multiple_of(512 * t, 512), 512)], NT,
                preferred_element_type=F32,
            )
            smoothed = p if smoothed is None else smoothed + p
        lo = jnp.concatenate([bound_lo[...]] * 4, axis=1)
        hi = jnp.concatenate([bound_hi[...]] * 4, axis=1)
        state[...] = jnp.minimum(jnp.maximum(state[...] - 0.02 * smoothed, lo), hi)
        for c in copies:
            c.wait_send()

    for s in range(8):
        final_send[s] = state[pl.ds(8 * s, 8), :]
    copies = []
    for k in range(1, 8):
        t, dev = at_plane(k)
        c = remote(final_send.at[t], final_recv.at[yx], plane_send_sem.at[3, k], plane_recv_sem.at[3, k], dev)
        c.start()
        copies.append(c)
    final_recv[yx] = final_send[yx]
    for c in copies:
        c.wait()
    for h in range(2):
        for a in range(4):
            parts = [final_recv[4 * h + c, :, pl.ds(128 * a, 128)] for c in range(4)]
            for b, y in enumerate(swap_blocks(parts, quarter8)):
                out[:, pl.ds(128 * (2 * (4 * a + b) + h), 128)] = y


def per_device(gains, response, student, blocks, order, lower, upper, lengths, amplitude):
    bounds = jnp.concatenate(
        [jnp.broadcast_to(lower[:, None], (8, 64)), jnp.broadcast_to(upper[:, None], (8, 64))], axis=1
    )
    vmem = pl.BlockSpec(memory_space=pltpu.VMEM)
    return pl.pallas_call(
        kernel,
        out_shape=jax.ShapeDtypeStruct((8, 4096), F32),
        in_specs=[vmem] * 8,
        out_specs=vmem,
        scratch_shapes=[
            pltpu.VMEM((8, 8, 640), F32),
            pltpu.VMEM((8, 8, 640), F32),
            pltpu.VMEM((64, 512), F32),
            pltpu.VMEM((64, 128), F32),
            pltpu.VMEM((64, 128), F32),
            pltpu.VMEM((16, 16, 128), BF16),
            pltpu.VMEM((ITERS, 16, 16, 128), BF16),
            pltpu.VMEM((16, 16, 128), BF16),
            pltpu.VMEM((ITERS, 16, 16, 128), BF16),
            pltpu.VMEM((ITERS, 8, 64, 512), BF16),
            pltpu.VMEM((8, 8, 512), F32),
            pltpu.VMEM((8, 8, 512), F32),
            pltpu.VMEM((1024, 1024), BF16),
            pltpu.VMEM((1024, 1024), BF16),
            pltpu.VMEM((256, 128), F32),
            pltpu.VMEM((256, 128), F32),
            pltpu.VMEM((256, 1024), BF16),
            pltpu.VMEM((512, 4096), BF16),
            pltpu.VMEM((8, 8, 128), F32),
            pltpu.VMEM((8, 8, 128), F32),
            pltpu.VMEM((4, 128, 128), F32),
            pltpu.VMEM((4, 128, 128), F32),
            pltpu.VMEM((128, 128), F32),
            pltpu.SemaphoreType.DMA((4, 8)),
            pltpu.SemaphoreType.DMA((4, 8)),
            pltpu.SemaphoreType.DMA((ITERS, 2, 16)),
            pltpu.SemaphoreType.DMA((ITERS, 2, 16)),
        ],
        compiler_params=pltpu.CompilerParams(collective_id=0, has_side_effects=True, vmem_limit_bytes=48 << 20),
        name="track",
    )(
        gains, bounds, response, student, blocks,
        order.reshape(8, 128), lengths.reshape(32, 128), amplitude.reshape(32, 128),
    )


def solution(mesh):
    placed = (
        P(("half", "wide"), None),
        P("wide", "half"),
        P("wide", "half"),
        P("half", None, None),
        P("half"),
        P(("half", "wide")),
        P(("half", "wide")),
        P(),
        P(),
    )
    return jax.shard_map(
        per_device, mesh=mesh, in_specs=placed, out_specs=P(("half", "wide"), None), check_vma=False
    )
```

time: 325 us -> 79.5 us (0.24)
  local copies, waits for them, and re-layouts: 112 us -> 7.07 us
  other arithmetic: 81.2 us -> 0.07 us
  Pallas kernels: 0 us -> 71.9 us
  blocking collectives: 51.8 us -> 0 us
  starting transfers between devices: 37.8 us -> 0 us
  matrix products: 30.1 us -> 0 us
  loops' own time: 10.2 us -> 0 us
    convert_element_type x17 -> x0, other arithmetic: 75 us -> none  [the longest x16 74 us: one_block(): return vals.astype(jnp.bfloat16)]
    pallas_call x0 -> x1, Pallas kernels: none -> 71.9 us  [per_device(): pl.pallas_call(kernel, out_shape=jax.ShapeDtypeStruct((8, 4096), F32), in...]
    dynamic_update_slice x32 -> x0, local copies, waits for them, and re-layouts: 70.1 us -> none  [covar_stack(): return lax.map(one_block, jnp.arange(count, dtype=jnp.int32))]
    all_to_all x2 -> x0, blocking collectives: 51.8 us -> none  [the longest x1 31.4 us: per_device(): lax.all_to_all(packed, 'wide', split_axis=1, concat_axis=0, tiled=True)]
    all_to_all x2 -> x0, starting transfers between devices: 37.8 us -> none  [the longest x1 20.6 us: per_device(): lax.all_to_all(packed, 'wide', split_axis=1, concat_axis=0, tiled=True)]
    dot_general x4 -> x0, matrix products: 30.1 us -> none  [the longest x2 29.6 us: per_device(): jnp.einsum('ce,bes->cbs', misfit, kernel_stack, preferred_element_type=jn...]
    gather x8 -> x0, local copies, waits for them, and re-layouts: 19.5 us -> none  [the longest x2 6.41 us: data_rows(): moved = jnp.take(packed, order, axis=1).reshape(rows, nblk, width)]
    dynamic_slice x32 -> x0, local copies, waits for them, and re-layouts: 10.6 us -> none  [the longest x16 9.44 us: covar_stack(): return lax.map(one_block, jnp.arange(count, dtype=jnp.int32))]
  transfers between devices with their start and end apart: 2 -> 0, of which waited for: 0 -> 0; matrix products, arithmetic and copies ran while one was open for 53% -> 0% of each run, Pallas kernels for 0% -> 0%
where the time goes in v1:
time: 79.5 us; the launch traced here: 79 us
  Pallas kernels  71.9 us (90%)
  local copies, waits for them, and re-layouts  7.07 us (9%)
    pallas_call x1, Pallas kernels, per_device(): pl.pallas_call(kernel, out_shape=jax.ShapeDtypeStruct((8, 4096), F32), in...  71.9 us
    unnamed x15, local copies, waits for them, and re-layouts  5.61 us

profile of v1, /device:TPU:4, one launch (start us, length us, event | category | flops | bytes accessed | tf_op | source)
XLA Modules:
  0.0 79.0 jit_solution(270637509519357585)
XLA Ops:
  0.0 0.0 copy-start.4
  0.0 0.7 broadcast_in_dim.4
  0.7 0.7 broadcast_in_dim.5
  1.5 0.0 copy-start.6
  1.5 0.1 pad_maximum_fusion.bounds
  1.5 0.0 copy-done.4
  1.5 0.6 copy-done.6
  2.2 0.0 copy-start
  2.2 1.0 %copy-done = bf16[4,256,256]{2,1,0:T(8,128)(2,1)S(1)} copy-done((bf16[4,256,256]{2,1,0:T(8,128)(2,1)S(1)}, bf16[4,256,256]{2,1,0:T(8,128)(2,1)}, u32[]{:S(2)}) %copy-start) | copy-done | bytes 524312
  3.2 0.0 copy-start.1
  3.2 0.9 %copy-done.1 = f32[8,4096]{1,0:T(8,128)S(1)} copy-done((f32[8,4096]{1,0:T(8,128)S(1)}, f32[8,4096]{1,0:T(8,128)}, u32[]{:S(2)}) %copy-start.1) | copy-done | bytes 131096
  4.1 0.0 copy-start.2
  4.1 0.8 %copy-done.2 = bf16[32,1024]{1,0:T(8,128)(2,1)S(1)} copy-done((bf16[32,1024]{1,0:T(8,128)(2,1)S(1)}, bf16[32,1024]{1,0:T(8,128)(2,1)}, u32[]{:S(2)}) %copy-start.2) | copy-done | bytes 65560
  4.9 0.0 copy-start.3
  4.9 0.8 %copy-done.3 = bf16[32,1024]{1,0:T(8,128)(2,1)S(1)} copy-done((bf16[32,1024]{1,0:T(8,128)(2,1)S(1)}, bf16[32,1024]{1,0:T(8,128)(2,1)}, u32[]{:S(2)}) %copy-start.3) | copy-done | bytes 65560
  5.8 0.0 copy-start.5
  5.8 0.7 copy-done.5
  6.5 71.9 %track.1 = f32[8,4096]{1,0:T(8,128)S(1)} custom-call(f32[8,4096]{1,0:T(8,128)S(1)} %copy-done.1, f32[8,128]{1,0:T(8,128)S(1)} %pad_maximum_fusion.bounds, bf16[32,1024]{1,0:T(8,128)(2,1)S(1)} %copy-done.2, bf16[32,1024]{1,0:T(8,128)(2,1)S(1)} %copy-done.3, bf16[4,256,256]{2,1,0:T(8,128)(2,1)S(1)} %copy-done, s32[8,128]{1,0:T(8,128)S(1)} %bitcast.5, ...), custom_call_target="tpu_custom_call" | custom-call | tf_op jit(solution)/shard_map/track/pallas_call | solution.py:247
  78.4 0.7 copy.11
Async XLA Ops:
  0.0 1.5 %copy-start.4 = (f32[4096]{0:T(1024)S(1)}, f32[4096]{0:T(1024)}, u32[]{:S(2)}) copy-start(f32[4096]{0:T(1024)} %param.16) | copy-start | bytes 49156
  1.5 0.7 copy-start.6
  2.2 1.0 %copy-start = (bf16[4,256,256]{2,1,0:T(8,128)(2,1)S(1)}, bf16[4,256,256]{2,1,0:T(8,128)(2,1)}, u32[]{:S(2)}) copy-start(bf16[4,256,256]{2,1,0:T(8,128)(2,1)} %blocks.1) | copy-start | bytes 1572868
  3.2 0.9 %copy-start.1 = (f32[8,4096]{1,0:T(8,128)S(1)}, f32[8,4096]{1,0:T(8,128)}, u32[]{:S(2)}) copy-start(f32[8,4096]{1,0:T(8,128)} %gains.1) | copy-start | bytes 393220
  4.1 0.8 %copy-start.2 = (bf16[32,1024]{1,0:T(8,128)(2,1)S(1)}, bf16[32,1024]{1,0:T(8,128)(2,1)}, u32[]{:S(2)}) copy-start(bf16[32,1024]{1,0:T(8,128)(2,1)} %response.1) | copy-start | bytes 196612
  4.9 0.8 %copy-start.3 = (bf16[32,1024]{1,0:T(8,128)(2,1)S(1)}, bf16[32,1024]{1,0:T(8,128)(2,1)}, u32[]{:S(2)}) copy-start(bf16[32,1024]{1,0:T(8,128)(2,1)} %student.1) | copy-start | bytes 196612
  5.8 0.7 copy-start.5

commit v2 on v1

v2 whole, which is shorter than its diff:
```python
import functools

import jax
import jax.numpy as jnp
from jax import lax
from jax.experimental import pallas as pl
from jax.experimental.pallas import tpu as pltpu
from jax.sharding import PartitionSpec as P

ITERS = 2
F32 = jnp.float32
BF16 = jnp.bfloat16
STEP = 4
NEAR = tuple(range(-STEP, 0)) + tuple(range(1, STEP + 1))
NT = (((1,), (1,)), ((), ()))


def swap_blocks(parts, quarter):
    out = []
    for b in range(4):
        acc = None
        for g in range(4):
            moved = parts[g] if g == b else pltpu.roll(parts[g], (32 * (g - b)) % 128, 1)
            acc = moved if acc is None else jnp.where(quarter == g, moved, acc)
        out.append(acc)
    return out


def kernel(
    gains_hbm, lower_hbm, upper_hbm, response_hbm, student_hbm, blocks_hbm, order_hbm, lengths_hbm, amplitude_hbm,
    out,
    gains, lower, upper, response, student, blocks, order, lengths, amplitude,
    start_send, start_recv, bound_send, bound_recv, state,
    pack_send, pack_recv, mis_send, mis_recv, gathered, final_send, final_recv,
    onehot, matrix, resp_tile, stud_tile, spread, covar, len_abs, amp_abs, len_rel, amp_rel, len_col, amp_col, pos_col,
    load_sem, entry_sem, plane_send_sem, plane_recv_sem, ag_send_sem, ag_recv_sem, col_send_sem, col_recv_sem,
):
    wide = lax.axis_index("wide")
    z = wide // 8
    yx = wide % 8

    def at_plane(k):
        t = (yx + k) % 8
        return t, {"wide": z * 8 + t}

    def at_column(k):
        t = (z + k + 16) % 16
        return t, {"wide": t * 8 + yx}

    def signal(sem, dev):
        pl.semaphore_signal(sem, inc=1, device_id=dev, device_id_type=pl.DeviceIdType.MESH)

    barrier = pltpu.get_barrier_semaphore()
    for k in NEAR:
        signal(barrier, at_column(k)[1])
    for k in range(1, 8):
        signal(barrier, at_plane(k)[1])

    loads = []
    for n, (src, dst) in enumerate((
        (gains_hbm, gains), (order_hbm, order), (blocks_hbm, blocks), (lower_hbm, lower), (upper_hbm, upper),
        (lengths_hbm, lengths), (amplitude_hbm, amplitude), (response_hbm, response), (student_hbm, student),
    )):
        c = pltpu.make_async_copy(src, dst, load_sem.at[n])
        c.start()
        loads.append(c)

    def remote(src, dst, ssem, rsem, dev):
        return pltpu.make_async_remote_copy(
            src_ref=src, dst_ref=dst, send_sem=ssem, recv_sem=rsem,
            device_id=dev, device_id_type=pl.DeviceIdType.MESH,
        )

    quarter8 = lax.broadcasted_iota(jnp.int32, (8, 128), 1) // 32
    quarter16 = lax.broadcasted_iota(jnp.int32, (16, 128), 1) // 32
    quarter256 = lax.broadcasted_iota(jnp.int32, (256, 128), 1) // 32

    loads[0].wait()
    for h in range(2):
        for a in range(4):
            parts = [gains[:, pl.ds(128 * (2 * (4 * a + b) + h), 128)] for b in range(4)]
            for c, y in enumerate(swap_blocks(parts, quarter8)):
                start_send[4 * h + c, :, pl.ds(128 * a, 128)] = y

    pl.semaphore_wait(barrier, 7 + len(NEAR))
    for k in (STEP, -STEP):
        signal(entry_sem, at_column(k)[1])

    starts = []
    for k in range(1, 8):
        t, dev = at_plane(k)
        c = remote(start_send.at[t], start_recv.at[yx], plane_send_sem.at[0, k], plane_recv_sem.at[0, k], dev)
        c.start()
        starts.append(c)
    start_recv[yx] = start_send[yx]

    loads[1].wait()
    row = lax.broadcasted_iota(jnp.int32, (1024, 128), 0)
    chan = ((row // 16) % 16) * 64 + (row // 256) * 16 + row % 16
    for j in range(8):
        onehot[:, pl.ds(128 * j, 128)] = jnp.where(chan == order[pl.ds(j, 1), :], 1.0, 0.0).astype(BF16)
    loads[2].wait()

    @pl.loop(0, 4)
    def _(q):
        rows = pl.ds(pl.multiple_of(q * 256, 256), 256)
        for b in range(4):
            spread[:, pl.ds(256 * b, 256)] = jnp.dot(
                onehot[rows, pl.ds(256 * b, 256)], blocks[b], preferred_element_type=F32
            ).astype(BF16)
        matrix[rows, :] = lax.dot_general(
            spread[...], onehot[...], NT, preferred_element_type=F32
        ).astype(BF16)

    for c in starts:
        c.wait()
    pl.semaphore_wait(entry_sem, 2)

    def send_column(it, which, send, recv, slot):
        copies = {}
        for k in (8, 7, 9, 6, 10, 5, 11, 4, 12, 3, 13, 2, 14, 1, 15):
            t, dev = at_column(k)
            c = remote(
                send.at[t], recv.at[it, slot(k)], col_send_sem.at[it, which, k], col_recv_sem.at[it, which, k], dev
            )
            c.start()
            copies[k] = c
        recv[it, slot(0)] = send[z]
        return copies

    def send_bounds():
        loads[3].wait()
        loads[4].wait()
        i0 = lax.broadcasted_iota(jnp.int32, (8, 128), 0)
        left = lax.broadcasted_iota(jnp.int32, (8, 128), 1) < 64
        tile = jnp.zeros((8, 128), F32)
        for r in range(8):
            tile = jnp.where(i0 == r, jnp.where(left, lower[r], upper[r]), tile)
        bound_send[...] = tile
        copies = []
        for k in range(1, 8):
            _, dev = at_plane(k)
            c = remote(bound_send, bound_recv.at[yx], plane_send_sem.at[1, k], plane_recv_sem.at[1, k], dev)
            c.start()
            copies.append(c)
        bound_recv[yx] = tile
        return copies

    def prepare_rest():
        loads[7].wait()
        loads[8].wait()
        for src, dst in ((response, resp_tile), (student, stud_tile)):
            x = src[...].astype(F32)
            tall = jnp.transpose(jnp.concatenate([x, x, x, x], axis=0))
            for t in range(16):
                acc = tall[64 * t : 64 * t + 16]
                for g in range(1, 4):
                    acc = jnp.where(quarter16 == g, tall[64 * t + 16 * g : 64 * t + 16 * g + 16], acc)
                dst[pl.ds(16 * t, 16), :] = acc

    def prepare_rows():
        loads[5].wait()
        loads[6].wait()
        quarter1 = lax.broadcasted_iota(jnp.int32, (1, 128), 1) // 32
        for src, dst in ((lengths, len_abs), (amplitude, amp_abs)):
            for h in range(2):
                for a in range(4):
                    parts = [src[pl.ds(h + 2 * b + 8 * a, 1), :] for b in range(4)]
                    for c, y in enumerate(swap_blocks(parts, quarter1)):
                        dst[pl.ds(4 * h + c, 1), pl.ds(128 * a, 128)] = y
        turn = ((4 - z + 16) % 16) * 32
        len_all = len_abs[...]
        amp_all = amp_abs[...] * jnp.sqrt(len_all)
        len_rel[...] = pltpu.roll(len_all * len_all, turn, 1)
        amp_rel[...] = pltpu.roll(amp_all, turn, 1)
        own_len = len_abs[pl.ds(yx, 1), :]
        own_amp = amp_abs[pl.ds(yx, 1), :]
        i0 = lax.broadcasted_iota(jnp.int32, (128, 128), 0)
        for a in range(4):
            lc = jnp.transpose(jnp.broadcast_to(own_len[:, 128 * a : 128 * a + 128], (128, 128)))
            ac = jnp.transpose(jnp.broadcast_to(own_amp[:, 128 * a : 128 * a + 128], (128, 128)))
            len_col[a] = lc * lc
            amp_col[a] = ac * jnp.sqrt(2.0 * lc)
            pos_col[a] = ((4 * a + i0 // 32) * 256 + i0 % 32 + yx * 32).astype(F32)

    def prepare_covar(first, last):
        i1 = lax.broadcasted_iota(jnp.int32, (1, 512), 1)
        pos = (((i1 // 32 + z + 12) % 16) * 256 + i1 % 32).astype(F32)

        @pl.loop(first, last)
        def _(t):
            lrow = len_rel[pl.ds(t, 1), :]
            arow = amp_rel[pl.ds(t, 1), :]
            prow = pos + (t * 32).astype(F32)
            for b in range(4):
                lr = lrow[:, 128 * b : 128 * b + 128]
                ar = arow[:, 128 * b : 128 * b + 128]
                pr = prow[:, 128 * b : 128 * b + 128]
                for a in range(4):
                    inv = lax.rsqrt(len_col[a] + lr)
                    q = (pos_col[a] - pr) * inv
                    vals = (amp_col[a] * ar) * (inv * jnp.exp(-(q * q)))
                    covar[pl.ds(128 * a, 128), pl.ds(pl.multiple_of(512 * t + 128 * b, 128), 128)] = vals.astype(BF16)

    def slot_of_plane(k):
        return z

    def slot_of_piece(k):
        return (4 - k) % 16

    for it in range(ITERS):
        now = start_recv[...].reshape(64, 512) if it == 0 else state[...]
        for a in range(4):
            parts = [now[16 * g : 16 * g + 16, 128 * a : 128 * a + 128] for g in range(4)]
            for b, y in enumerate(swap_blocks(parts, quarter16)):
                pack_send[4 * a + b] = y.astype(BF16)
        copies = send_column(it, 0, pack_send, pack_recv, slot_of_plane)
        if it == 0:
            bounds = send_bounds()
            prepare_rest()
            prepare_rows()
            prepare_covar(0, 3)
        for c in copies.values():
            c.wait()
        got = pack_recv[it].astype(F32).reshape(256, 128)
        for g in range(4):
            x = jnp.where(quarter256 == g, got, 0.0)
            x = x + pltpu.roll(x, 32, 1)
            x = x + pltpu.roll(x, 64, 1)
            spread[:, pl.ds(128 * g, 128)] = x.astype(BF16)
        prod = None
        for g2 in range(4):
            acc = None
            for g in range(4):
                p = jnp.dot(
                    matrix[pl.ds(256 * g2, 256), pl.ds(256 * g, 256)], spread[:, pl.ds(128 * g, 128)],
                    preferred_element_type=F32,
                )
                acc = p if acc is None else acc + p
            prod = acc if prod is None else jnp.where(quarter256 == g2, acc, prod)
        misfit = (stud_tile[...] * (prod - resp_tile[...])).astype(BF16)
        mis_send[...] = misfit.reshape(16, 16, 128)
        copies = send_column(it, 1, mis_send, mis_recv, slot_of_piece)
        if it == 0:
            prepare_covar(3, 6)

        forwards = []
        for part in range(2):
            for k, c in copies.items():
                if slot_of_piece(k) // 8 == part:
                    c.wait_recv()
            for a in range(2):
                parts = [mis_recv[it, 8 * part + 4 * a + b].astype(F32) for b in range(4)]
                for g, y in enumerate(swap_blocks(parts, quarter16)):
                    gathered[it, yx, part, pl.ds(16 * g, 16), pl.ds(128 * a, 128)] = y.astype(BF16)
            sent = []
            for k in range(1, 8):
                t, dev = at_plane(k)
                c = remote(
                    gathered.at[it, yx, part], gathered.at[it, yx, part],
                    ag_send_sem.at[it, part, k], ag_recv_sem.at[it, part, k], dev,
                )
                c.start()
                sent.append(c)
            forwards.append(sent)
            if it == 0 and part == 0:
                prepare_covar(6, 8)

        smoothed = None
        for part in range(2):
            for k in range(8):
                if k:
                    forwards[part][k - 1].wait_recv()
                t = (yx - k + 8) % 8
                p = lax.dot_general(
                    gathered[it, t, part], covar[:, pl.ds(pl.multiple_of(512 * t + 256 * part, 256), 256)], NT,
                    preferred_element_type=F32,
                )
                smoothed = p if smoothed is None else smoothed + p
        if it == 0:
            for c in bounds:
                c.wait()
        edge = bound_recv[...].reshape(64, 128)
        lo = jnp.broadcast_to(edge[:, 0:1], (64, 512))
        hi = jnp.broadcast_to(edge[:, 64:65], (64, 512))
        now = start_recv[...].reshape(64, 512) if it == 0 else state[...]
        nxt = jnp.minimum(jnp.maximum(now - 0.02 * smoothed, lo), hi)
        if it < ITERS - 1:
            state[...] = nxt
        else:
            final_send[...] = nxt.reshape(8, 8, 512)
        for c in copies.values():
            c.wait_send()
        for sent in forwards:
            for c in sent:
                c.wait_send()

    copies = []
    for k in range(1, 8):
        t, dev = at_plane(k)
        c = remote(final_send.at[t], final_recv.at[yx], plane_send_sem.at[2, k], plane_recv_sem.at[2, k], dev)
        c.start()
        copies.append(c)
    final_recv[yx] = final_send[yx]
    for c in copies:
        c.wait()
    for h in range(2):
        for a in range(4):
            parts = [final_recv[4 * h + c, :, pl.ds(128 * a, 128)] for c in range(4)]
            for b, y in enumerate(swap_blocks(parts, quarter8)):
                out[:, pl.ds(128 * (2 * (4 * a + b) + h), 128)] = y


def per_device(gains, response, student, blocks, order, lower, upper, lengths, amplitude):
    hbm = pl.BlockSpec(memory_space=pltpu.HBM)
    return pl.pallas_call(
        kernel,
        out_shape=jax.ShapeDtypeStruct((8, 4096), F32),
        in_specs=[hbm] * 9,
        out_specs=pl.BlockSpec(memory_space=pltpu.VMEM),
        scratch_shapes=[
            pltpu.VMEM((8, 4096), F32),
            pltpu.SMEM((8,), F32),
            pltpu.SMEM((8,), F32),
            pltpu.VMEM((32, 1024), BF16),
            pltpu.VMEM((32, 1024), BF16),
            pltpu.VMEM((4, 256, 256), BF16),
            pltpu.VMEM((8, 128), jnp.int32),
            pltpu.VMEM((32, 128), F32),
            pltpu.VMEM((32, 128), F32),
            pltpu.VMEM((8, 8, 512), F32),
            pltpu.VMEM((8, 8, 512), F32),
            pltpu.VMEM((8, 128), F32),
            pltpu.VMEM((8, 8, 128), F32),
            pltpu.VMEM((64, 512), F32),
            pltpu.VMEM((16, 16, 128), BF16),
            pltpu.VMEM((ITERS, 16, 16, 128), BF16),
            pltpu.VMEM((16, 16, 128), BF16),
            pltpu.VMEM((ITERS, 16, 16, 128), BF16),
            pltpu.VMEM((ITERS, 8, 2, 64, 256), BF16),
            pltpu.VMEM((8, 8, 512), F32),
            pltpu.VMEM((8, 8, 512), F32),
            pltpu.VMEM((1024, 1024), BF16),
            pltpu.VMEM((1024, 1024), BF16),
            pltpu.VMEM((256, 128), F32),
            pltpu.VMEM((256, 128), F32),
            pltpu.VMEM((256, 1024), BF16),
            pltpu.VMEM((512, 4096), BF16),
            pltpu.VMEM((8, 512), F32),
            pltpu.VMEM((8, 512), F32),
            pltpu.VMEM((8, 512), F32),
            pltpu.VMEM((8, 512), F32),
            pltpu.VMEM((4, 128, 128), F32),
            pltpu.VMEM((4, 128, 128), F32),
            pltpu.VMEM((4, 128, 128), F32),
            pltpu.SemaphoreType.DMA((9,)),
            pltpu.SemaphoreType.REGULAR,
            pltpu.SemaphoreType.DMA((3, 8)),
            pltpu.SemaphoreType.DMA((3, 8)),
            pltpu.SemaphoreType.DMA((ITERS, 2, 8)),
            pltpu.SemaphoreType.DMA((ITERS, 2, 8)),
            pltpu.SemaphoreType.DMA((ITERS, 2, 16)),
            pltpu.SemaphoreType.DMA((ITERS, 2, 16)),
        ],
        compiler_params=pltpu.CompilerParams(collective_id=0, has_side_effects=True, vmem_limit_bytes=24 << 20),
        name="track",
    )(
        gains, lower, upper, response, student, blocks,
        order.reshape(8, 128), lengths.reshape(32, 128), amplitude.reshape(32, 128),
    )


def solution(mesh):
    placed = (
        P(("half", "wide"), None),
        P("wide", "half"),
        P("wide", "half"),
        P("half", None, None),
        P("half"),
        P(("half", "wide")),
        P(("half", "wide")),
        P(),
        P(),
    )
    return jax.shard_map(
        per_device, mesh=mesh, in_specs=placed, out_specs=P(("half", "wide"), None), check_vma=False
    )
```

time: 79.5 us -> 72.6 us (0.913)
  the two profiles are of different devices: /device:TPU:4 before, /device:TPU:2 now
where the time goes in v2:
time: 72.6 us; the launch traced here: 72.2 us
  Pallas kernels  65.8 us (91%)
  local copies, waits for them, and re-layouts  6.4 us (9%)
    pallas_call x1, Pallas kernels, per_device(): pl.pallas_call(kernel, out_shape=jax.ShapeDtypeStruct((8, 4096), F32), in...  65.8 us
    unnamed x19, local copies, waits for them, and re-layouts  6.4 us

profile of v2, /device:TPU:2, one launch (start us, length us, event | category | flops | bytes accessed | tf_op | source)
XLA Modules:
  0.0 72.2 jit_solution(9683469457293366363)
XLA Ops:
  0.0 0.0 copy-start.6
  0.0 0.0 copy-start.7
  0.0 0.0 copy-start.8
  0.0 0.7 copy-done.6
  0.7 0.0 copy-done.7
  0.7 0.0 copy-done.8
  0.7 0.0 copy-start
  0.7 1.0 %copy-done = bf16[4,256,256]{2,1,0:T(8,128)(2,1)S(1)} copy-done((bf16[4,256,256]{2,1,0:T(8,128)(2,1)S(1)}, bf16[4,256,256]{2,1,0:T(8,128)(2,1)}, u32[]{:S(2)}) %copy-start) | copy-done | bytes 524312
  1.7 0.0 copy-start.1
  1.7 0.9 %copy-done.1 = f32[8,4096]{1,0:T(8,128)S(1)} copy-done((f32[8,4096]{1,0:T(8,128)S(1)}, f32[8,4096]{1,0:T(8,128)}, u32[]{:S(2)}) %copy-start.1) | copy-done | bytes 131096
  2.6 0.0 copy-start.2
  2.6 0.8 %copy-done.2 = bf16[32,1024]{1,0:T(8,128)(2,1)S(1)} copy-done((bf16[32,1024]{1,0:T(8,128)(2,1)S(1)}, bf16[32,1024]{1,0:T(8,128)(2,1)}, u32[]{:S(2)}) %copy-start.2) | copy-done | bytes 65560
  3.5 0.0 copy-start.3
  3.5 0.8 %copy-done.3 = bf16[32,1024]{1,0:T(8,128)(2,1)S(1)} copy-done((bf16[32,1024]{1,0:T(8,128)(2,1)S(1)}, bf16[32,1024]{1,0:T(8,128)(2,1)}, u32[]{:S(2)}) %copy-start.3) | copy-done | bytes 65560
  4.3 0.0 copy-start.4
  4.3 0.7 copy-done.4
  5.0 0.0 copy-start.5
  5.0 0.7 copy-done.5
  5.8 65.8 %track.1 = f32[8,4096]{1,0:T(8,128)S(1)} custom-call(f32[8,4096]{1,0:T(8,128)S(1)} %copy-done.1, f32[8]{0:T(128)S(1)} %copy-done.7, f32[8]{0:T(128)S(1)} %copy-done.8, bf16[32,1024]{1,0:T(8,128)(2,1)S(1)} %copy-done.2, bf16[32,1024]{1,0:T(8,128)(2,1)S(1)} %copy-done.3, bf16[4,256,256]{2,1,0:T(8,128)(2,1)S(1)} %copy-done, s32[8,128]{1,0:T(8,128)S(1)} %bitcast.5, ...), custom_call_target="tpu_custom_call" | custom-call | tf_op jit(solution)/shard_map/track/pallas_call | solution.py:316
  71.5 0.7 copy.11
Async XLA Ops:
  0.0 0.7 copy-start.6
  0.0 0.7 copy-start.7
  0.0 0.7 copy-start.8
  0.7 1.0 %copy-start = (bf16[4,256,256]{2,1,0:T(8,128)(2,1)S(1)}, bf16[4,256,256]{2,1,0:T(8,128)(2,1)}, u32[]{:S(2)}) copy-start(bf16[4,256,256]{2,1,0:T(8,128)(2,1)} %blocks_hbm.1) | copy-start | bytes 1572868
  1.7 0.9 %copy-start.1 = (f32[8,4096]{1,0:T(8,128)S(1)}, f32[8,4096]{1,0:T(8,128)}, u32[]{:S(2)}) copy-start(f32[8,4096]{1,0:T(8,128)} %gains_hbm.1) | copy-start | bytes 393220
  2.6 0.8 %copy-start.2 = (bf16[32,1024]{1,0:T(8,128)(2,1)S(1)}, bf16[32,1024]{1,0:T(8,128)(2,1)}, u32[]{:S(2)}) copy-start(bf16[32,1024]{1,0:T(8,128)(2,1)} %response_hbm.1) | copy-start | bytes 196612
  3.5 0.8 %copy-start.3 = (bf16[32,1024]{1,0:T(8,128)(2,1)S(1)}, bf16[32,1024]{1,0:T(8,128)(2,1)}, u32[]{:S(2)}) copy-start(bf16[32,1024]{1,0:T(8,128)(2,1)} %student_hbm.1) | copy-start | bytes 196612
  4.3 0.7 copy-start.4
  5.0 0.7 copy-start.5

commit v3 on v2

--- a/solution.py
+++ b/solution.py
@@ -10,8 +10,11 @@
 ITERS = 2
 F32 = jnp.float32
 BF16 = jnp.bfloat16
-STEP = 4
-NEAR = tuple(range(-STEP, 0)) + tuple(range(1, STEP + 1))
+NEAR = (-4, 4, -3, 3, -2, 2, -1, 1)
+FAR = (8, 7, 9, 6, 10, 5, 11, 4)
+CLOSE = (12, 3, 13, 2, 14, 1, 15)
+PLANE = (5, 4, 3, 7, 2, 6, 1)
+FROM = (0, 1, -2, -1, -4, -3, 2, 3, 4, 5, -6, -5, -8, -7, 6, 7)
 NT = (((1,), (1,)), ((), ()))
 
 
@@ -32,15 +35,15 @@
     gains, lower, upper, response, student, blocks, order, lengths, amplitude,
     start_send, start_recv, bound_send, bound_recv, state,
     pack_send, pack_recv, mis_send, mis_recv, gathered, final_send, final_recv,
-    onehot, matrix, resp_tile, stud_tile, spread, covar, len_abs, amp_abs, len_rel, amp_rel, len_col, amp_col, pos_col,
+    onehot, matrix, moved, partial, tall, resp_tile, stud_tile, spread, covar, len_abs, amp_abs, len_rel, amp_rel, len_col, amp_col, pos_col,
     load_sem, entry_sem, plane_send_sem, plane_recv_sem, ag_send_sem, ag_recv_sem, col_send_sem, col_recv_sem,
 ):
     wide = lax.axis_index("wide")
     z = wide // 8
     yx = wide % 8
 
-    def at_plane(k):
-        t = (yx + k) % 8
+    def at_plane(k, sign=1):
+        t = ((yx // 2 + sign * (k // 2) + 4) % 4) * 2 + (yx % 2 + k) % 2
         return t, {"wide": z * 8 + t}
 
     def at_column(k):
@@ -53,7 +56,7 @@
     barrier = pltpu.get_barrier_semaphore()
     for k in NEAR:
         signal(barrier, at_column(k)[1])
-    for k in range(1, 8):
+    for k in PLANE:
         signal(barrier, at_plane(k)[1])
 
     loads = []
@@ -73,7 +76,7 @@
 
     quarter8 = lax.broadcasted_iota(jnp.int32, (8, 128), 1) // 32
     quarter16 = lax.broadcasted_iota(jnp.int32, (16, 128), 1) // 32
-    quarter256 = lax.broadcasted_iota(jnp.int32, (256, 128), 1) // 32
+    quarter128 = lax.broadcasted_iota(jnp.int32, (128, 128), 1) // 32
 
     loads[0].wait()
     for h in range(2):
@@ -83,11 +86,11 @@
                 start_send[4 * h + c, :, pl.ds(128 * a, 128)] = y
 
     pl.semaphore_wait(barrier, 7 + len(NEAR))
-    for k in (STEP, -STEP):
+    for k in (4, -4):
         signal(entry_sem, at_column(k)[1])
 
     starts = []
-    for k in range(1, 8):
+    for k in PLANE:
         t, dev = at_plane(k)
         c = remote(start_send.at[t], start_recv.at[yx], plane_send_sem.at[0, k], plane_recv_sem.at[0, k], dev)
         c.start()
@@ -96,7 +99,7 @@
 
     loads[1].wait()
     row = lax.broadcasted_iota(jnp.int32, (1024, 128), 0)
-    chan = ((row // 16) % 16) * 64 + (row // 256) * 16 + row % 16
+    chan = ((z + 12 + (row // 512) * 8 + (row // 16) % 8) % 16) * 64 + ((row // 128) % 4) * 16 + row % 16
     for j in range(8):
         onehot[:, pl.ds(128 * j, 128)] = jnp.where(chan == order[pl.ds(j, 1), :], 1.0, 0.0).astype(BF16)
     loads[2].wait()
@@ -116,17 +119,15 @@
         c.wait()
     pl.semaphore_wait(entry_sem, 2)
 
-    def send_column(it, which, send, recv, slot):
-        copies = {}
-        for k in (8, 7, 9, 6, 10, 5, 11, 4, 12, 3, 13, 2, 14, 1, 15):
+    def send_column(copies, ks, it, which, send, at_send, recv, at_recv):
+        for k in ks:
             t, dev = at_column(k)
             c = remote(
-                send.at[t], recv.at[it, slot(k)], col_send_sem.at[it, which, k], col_recv_sem.at[it, which, k], dev
+                send.at[at_send(k)], recv.at[it, at_recv(k)],
+                col_send_sem.at[it, which, k], col_recv_sem.at[it, which, k], dev,
             )
             c.start()
             copies[k] = c
-        recv[it, slot(0)] = send[z]
-        return copies
 
     def send_bounds():
         loads[3].wait()
@@ -138,7 +139,7 @@
             tile = jnp.where(i0 == r, jnp.where(left, lower[r], upper[r]), tile)
         bound_send[...] = tile
         copies = []
-        for k in range(1, 8):
+        for k in PLANE:
             _, dev = at_plane(k)
             c = remote(bound_send, bound_recv.at[yx], plane_send_sem.at[1, k], plane_recv_sem.at[1, k], dev)
             c.start()
@@ -151,12 +152,20 @@
         loads[8].wait()
         for src, dst in ((response, resp_tile), (student, stud_tile)):
             x = src[...].astype(F32)
-            tall = jnp.transpose(jnp.concatenate([x, x, x, x], axis=0))
-            for t in range(16):
-                acc = tall[64 * t : 64 * t + 16]
+            tall[...] = jnp.transpose(jnp.concatenate([x, x, x, x], axis=0))
+            for s in range(16):
+                first = ((z + 12 + s) % 16) * 64
+                acc = tall[pl.ds(pl.multiple_of(first, 64), 16), :]
                 for g in range(1, 4):
-                    acc = jnp.where(quarter16 == g, tall[64 * t + 16 * g : 64 * t + 16 * g + 16], acc)
-                dst[pl.ds(16 * t, 16), :] = acc
+                    acc = jnp.where(quarter16 == g, tall[pl.ds(pl.multiple_of(first + 16 * g, 16), 16), :], acc)
+                dst[pl.ds(16 * s, 16), :] = acc
+
+    def by_slot(x):
+        v = [x[:, 128 * n : 128 * n + 128] for n in range(4)]
+        left = lax.broadcasted_iota(jnp.int32, v[0].shape, 1) < 64
+        return jnp.concatenate(
+            [jnp.where(left, v[a], v[b]) for a, b in ((2, 1), (1, 2), (3, 0), (0, 3))], axis=1
+        )
 
     def prepare_rows():
         loads[5].wait()
@@ -168,11 +177,11 @@
                     parts = [src[pl.ds(h + 2 * b + 8 * a, 1), :] for b in range(4)]
                     for c, y in enumerate(swap_blocks(parts, quarter1)):
                         dst[pl.ds(4 * h + c, 1), pl.ds(128 * a, 128)] = y
-        turn = ((4 - z + 16) % 16) * 32
+        turn = ((24 - z) % 16) * 32
         len_all = len_abs[...]
         amp_all = amp_abs[...] * jnp.sqrt(len_all)
-        len_rel[...] = pltpu.roll(len_all * len_all, turn, 1)
-        amp_rel[...] = pltpu.roll(amp_all, turn, 1)
+        len_rel[...] = by_slot(pltpu.roll(len_all * len_all, turn, 1))
+        amp_rel[...] = by_slot(pltpu.roll(amp_all, turn, 1))
         own_len = len_abs[pl.ds(yx, 1), :]
         own_amp = amp_abs[pl.ds(yx, 1), :]
         i0 = lax.broadcasted_iota(jnp.int32, (128, 128), 0)
@@ -185,7 +194,7 @@
 
     def prepare_covar(first, last):
         i1 = lax.broadcasted_iota(jnp.int32, (1, 512), 1)
-        pos = (((i1 // 32 + z + 12) % 16) * 256 + i1 % 32).astype(F32)
+        pos = by_slot((((i1 // 32 + z + 8) % 16) * 256 + i1 % 32).astype(F32))
 
         @pl.loop(first, last)
         def _(t):
@@ -202,11 +211,17 @@
                     vals = (amp_col[a] * ar) * (inv * jnp.exp(-(q * q)))
                     covar[pl.ds(128 * a, 128), pl.ds(pl.multiple_of(512 * t + 128 * b, 128), 128)] = vals.astype(BF16)
 
-    def slot_of_plane(k):
-        return z
+    def plane_of(k):
+        return (z + k) % 16
+
+    def order_of(k):
+        return (k + 4) % 16
+
+    def order_from(k):
+        return (4 - k) % 16
 
     def slot_of_piece(k):
-        return (4 - k) % 16
+        return FROM.index((8 - k) % 16 - 8)
 
     for it in range(ITERS):
         now = start_recv[...].reshape(64, 512) if it == 0 else state[...]
@@ -214,47 +229,61 @@
             parts = [now[16 * g : 16 * g + 16, 128 * a : 128 * a + 128] for g in range(4)]
             for b, y in enumerate(swap_blocks(parts, quarter16)):
                 pack_send[4 * a + b] = y.astype(BF16)
-        copies = send_column(it, 0, pack_send, pack_recv, slot_of_plane)
+        copies = {}
+        send_column(copies, FAR + CLOSE, it, 0, pack_send, plane_of, pack_recv, order_from)
+        pack_recv[it, 4] = pack_send[z]
         if it == 0:
             bounds = send_bounds()
             prepare_rest()
             prepare_rows()
-            prepare_covar(0, 3)
+            prepare_covar(0, 4)
+
+        def take(half):
+            got = pack_recv[it, pl.ds(8 * half, 8)].astype(F32).reshape(128, 128)
+            for g in range(4):
+                x = jnp.where(quarter128 == g, got, 0.0)
+                x = x + pltpu.roll(x, 32, 1)
+                x = x + pltpu.roll(x, 64, 1)
+                moved[pl.ds(512 * half + 128 * g, 128), :] = x.astype(BF16)
+
+        for k, c in copies.items():
+            if order_from(k) < 8:
+                c.wait_recv()
+        take(0)
+        partial[...] = jnp.dot(matrix[:, pl.ds(0, 512)], moved[pl.ds(0, 512), :], preferred_element_type=F32)
+        for k, c in copies.items():
+            if order_from(k) >= 8:
+                c.wait_recv()
+        take(1)
         for c in copies.values():
-            c.wait()
-        got = pack_recv[it].astype(F32).reshape(256, 128)
-        for g in range(4):
-            x = jnp.where(quarter256 == g, got, 0.0)
-            x = x + pltpu.roll(x, 32, 1)
-            x = x + pltpu.roll(x, 64, 1)
-            spread[:, pl.ds(128 * g, 128)] = x.astype(BF16)
-        prod = None
-        for g2 in range(4):
-            acc = None
-            for g in range(4):
-                p = jnp.dot(
-                    matrix[pl.ds(256 * g2, 256), pl.ds(256 * g, 256)], spread[:, pl.ds(128 * g, 128)],
-                    preferred_element_type=F32,
-                )
-                acc = p if acc is None else acc + p
-            prod = acc if prod is None else jnp.where(quarter256 == g2, acc, prod)
-        misfit = (stud_tile[...] * (prod - resp_tile[...])).astype(BF16)
-        mis_send[...] = misfit.reshape(16, 16, 128)
-        copies = send_column(it, 1, mis_send, mis_recv, slot_of_piece)
+            c.wait_send()
+        copies = {}
+        for half, ks in ((1, FAR), (0, CLOSE)):
+            rows = pl.ds(512 * half, 512)
+            full = partial[rows, :] + jnp.dot(
+                matrix[rows, pl.ds(512, 512)], moved[pl.ds(512, 512), :], preferred_element_type=F32
+            )
+            prod = full[0:128]
+            for g in range(1, 4):
+                prod = jnp.where(quarter128 == g, full[128 * g : 128 * g + 128], prod)
+            own = pl.ds(128 * half, 128)
+            misfit = (stud_tile[own, :] * (prod - resp_tile[own, :])).astype(BF16)
+            mis_send[pl.ds(8 * half, 8)] = misfit.reshape(8, 16, 128)
+            send_column(copies, ks, it, 1, mis_send, order_of, mis_recv, slot_of_piece)
+        mis_recv[it, slot_of_piece(0)] = mis_send[4]
         if it == 0:
-            prepare_covar(3, 6)
+            prepare_covar(4, 6)
 
         forwards = []
-        for part in range(2):
+        for part in range(4):
             for k, c in copies.items():
-                if slot_of_piece(k) // 8 == part:
+                if slot_of_piece(k) // 4 == part:
                     c.wait_recv()
-            for a in range(2):
-                parts = [mis_recv[it, 8 * part + 4 * a + b].astype(F32) for b in range(4)]
-                for g, y in enumerate(swap_blocks(parts, quarter16)):
-                    gathered[it, yx, part, pl.ds(16 * g, 16), pl.ds(128 * a, 128)] = y.astype(BF16)
+            parts = [mis_recv[it, 4 * part + b].astype(F32) for b in range(4)]
+            for g, y in enumerate(swap_blocks(parts, quarter16)):
+                gathered[it, yx, part, pl.ds(16 * g, 16), :] = y.astype(BF16)
             sent = []
-            for k in range(1, 8):
+            for k in PLANE:
                 t, dev = at_plane(k)
                 c = remote(
                     gathered.at[it, yx, part], gathered.at[it, yx, part],
@@ -263,18 +292,24 @@
                 c.start()
                 sent.append(c)
             forwards.append(sent)
-            if it == 0 and part == 0:
-                prepare_covar(6, 8)
+            if it == 0 and part == 1:
+                prepare_covar(6, 7)
+        if it == 0:
+            prepare_covar(7, 8)
 
         smoothed = None
-        for part in range(2):
-            for k in range(8):
-                if k:
-                    forwards[part][k - 1].wait_recv()
-                t = (yx - k + 8) % 8
+        for parts in ((0, 1), (2,), (3,)):
+            for n in range(0, 8, 3 - len(parts)):
+                left, right = [], []
+                for m in range(n, n + 3 - len(parts)):
+                    t = at_plane(PLANE[-m], -1)[0] if m else yx
+                    for part in parts:
+                        if m:
+                            forwards[part][-m].wait_recv()
+                        left.append(gathered[it, t, part])
+                        right.append(covar[:, pl.ds(pl.multiple_of(512 * t + 128 * part, 128), 128)])
                 p = lax.dot_general(
-                    gathered[it, t, part], covar[:, pl.ds(pl.multiple_of(512 * t + 256 * part, 256), 256)], NT,
-                    preferred_element_type=F32,
+                    jnp.concatenate(left, axis=1), jnp.concatenate(right, axis=1), NT, preferred_element_type=F32
                 )
                 smoothed = p if smoothed is None else smoothed + p
         if it == 0:
@@ -296,7 +331,7 @@
                 c.wait_send()
 
     copies = []
-    for k in range(1, 8):
+    for k in PLANE:
         t, dev = at_plane(k)
         c = remote(final_send.at[t], final_recv.at[yx], plane_send_sem.at[2, k], plane_recv_sem.at[2, k], dev)
         c.start()
@@ -337,11 +372,14 @@
             pltpu.VMEM((ITERS, 16, 16, 128), BF16),
             pltpu.VMEM((16, 16, 128), BF16),
             pltpu.VMEM((ITERS, 16, 16, 128), BF16),
-            pltpu.VMEM((ITERS, 8, 2, 64, 256), BF16),
+            pltpu.VMEM((ITERS, 8, 4, 64, 128), BF16),
             pltpu.VMEM((8, 8, 512), F32),
             pltpu.VMEM((8, 8, 512), F32),
             pltpu.VMEM((1024, 1024), BF16),
             pltpu.VMEM((1024, 1024), BF16),
+            pltpu.VMEM((1024, 128), BF16),
+            pltpu.VMEM((1024, 128), F32),
+            pltpu.VMEM((1024, 128), F32),
             pltpu.VMEM((256, 128), F32),
             pltpu.VMEM((256, 128), F32),
             pltpu.VMEM((256, 1024), BF16),
@@ -357,17 +395,20 @@
             pltpu.SemaphoreType.REGULAR,
             pltpu.SemaphoreType.DMA((3, 8)),
             pltpu.SemaphoreType.DMA((3, 8)),
-            pltpu.SemaphoreType.DMA((ITERS, 2, 8)),
-            pltpu.SemaphoreType.DMA((ITERS, 2, 8)),
+            pltpu.SemaphoreType.DMA((ITERS, 4, 8)),
+            pltpu.SemaphoreType.DMA((ITERS, 4, 8)),
             pltpu.SemaphoreType.DMA((ITERS, 2, 16)),
             pltpu.SemaphoreType.DMA((ITERS, 2, 16)),
         ],
         compiler_params=pltpu.CompilerParams(collective_id=0, has_side_effects=True, vmem_limit_bytes=24 << 20),
         name="track",
-    )(
-        gains, lower, upper, response, student, blocks,
-        order.reshape(8, 128), lengths.reshape(32, 128), amplitude.reshape(32, 128),
-    )
+    )(*[
+        pltpu.with_memory_space_constraint(v, pltpu.HBM)
+        for v in (
+            gains, lower, upper, response, student, blocks,
+            order.reshape(8, 128), lengths.reshape(32, 128), amplitude.reshape(32, 128),
+        )
+    ])
 
 
 def solution(mesh):

time: 72.6 us -> 65.4 us (0.901)
  the two profiles are of different devices: /device:TPU:2 before, /device:TPU:4 now
where the time goes in v3:
time: 65.4 us; the launch traced here: 65.3 us
  Pallas kernels  64.6 us (99%)
  local copies, waits for them, and re-layouts  0.66 us (1%)
    pallas_call x1, Pallas kernels, per_device(): pl.pallas_call(kernel, out_shape=jax.ShapeDtypeStruct((8, 4096), F32), in...  64.6 us

profile of v3, /device:TPU:4, one launch (start us, length us, event | category | flops | bytes accessed | tf_op | source)
XLA Modules:
  0.0 65.3 jit_solution(10922655195471388974)
XLA Ops:
  0.0 64.6 %track.1 = f32[8,4096]{1,0:T(8,128)S(1)} custom-call(f32[8,4096]{1,0:T(8,128)} %gains_hbm.1, f32[8]{0:T(128)} %lower_hbm.1, f32[8]{0:T(128)} %upper_hbm.1, bf16[32,1024]{1,0:T(8,128)(2,1)} %response_hbm.1, bf16[32,1024]{1,0:T(8,128)(2,1)} %student_hbm.1, bf16[4,256,256]{2,1,0:T(8,128)(2,1)} %blocks_hbm.1, s32[8,128]{1,0:T(8,128)} %bitcast.5, ...), custom_call_target="tpu_custom_call" | custom-call | tf_op jit(solution)/shard_map/track/pallas_call | solution.py:351
  64.6 0.7 %copy.11 = f32[8,4096]{1,0:T(8,128)} copy(f32[8,4096]{1,0:T(8,128)S(1)} %track.1) | data formatting | bytes 262144

commit v4 on v3

--- a/solution.py
+++ b/solution.py
@@ -35,7 +35,7 @@
     gains, lower, upper, response, student, blocks, order, lengths, amplitude,
     start_send, start_recv, bound_send, bound_recv, state,
     pack_send, pack_recv, mis_send, mis_recv, gathered, final_send, final_recv,
-    onehot, matrix, moved, partial, tall, resp_tile, stud_tile, spread, covar, len_abs, amp_abs, len_rel, amp_rel, len_col, amp_col, pos_col,
+    onehot, matrix, moved, partial, tall, resp_tile, stud_tile, spread, covar, len_abs, amp_abs, own_row, len_col, amp_col, pos_col,
     load_sem, entry_sem, plane_send_sem, plane_recv_sem, ag_send_sem, ag_recv_sem, col_send_sem, col_recv_sem,
 ):
     wide = lax.axis_index("wide")
@@ -180,36 +180,35 @@
         turn = ((24 - z) % 16) * 32
         len_all = len_abs[...]
         amp_all = amp_abs[...] * jnp.sqrt(len_all)
-        len_rel[...] = by_slot(pltpu.roll(len_all * len_all, turn, 1))
-        amp_rel[...] = by_slot(pltpu.roll(amp_all, turn, 1))
+        i1 = lax.broadcasted_iota(jnp.int32, (8, 512), 1)
+        sq = by_slot(pltpu.roll(len_all * len_all, turn, 1))
+        am = by_slot(pltpu.roll(amp_all, turn, 1))
+        ps = by_slot((((i1 // 32 + z + 8) % 16) * 256 + i1 % 32).astype(F32))
+        for b in range(4):
+            part = slice(128 * b, 128 * b + 128)
+            sq_t, am_t, ps_t = jnp.transpose(sq[:, part]), jnp.transpose(am[:, part]), jnp.transpose(ps[:, part])
+            pos_col[b] = jnp.broadcast_to(ps_t[:, 0:1], (128, 128))
+            for t in range(8):
+                len_col[t, b] = jnp.broadcast_to(sq_t[:, t : t + 1], (128, 128))
+                amp_col[t, b] = jnp.broadcast_to(am_t[:, t : t + 1], (128, 128))
         own_len = len_abs[pl.ds(yx, 1), :]
         own_amp = amp_abs[pl.ds(yx, 1), :]
-        i0 = lax.broadcasted_iota(jnp.int32, (128, 128), 0)
-        for a in range(4):
-            lc = jnp.transpose(jnp.broadcast_to(own_len[:, 128 * a : 128 * a + 128], (128, 128)))
-            ac = jnp.transpose(jnp.broadcast_to(own_amp[:, 128 * a : 128 * a + 128], (128, 128)))
-            len_col[a] = lc * lc
-            amp_col[a] = ac * jnp.sqrt(2.0 * lc)
-            pos_col[a] = ((4 * a + i0 // 32) * 256 + i0 % 32 + yx * 32).astype(F32)
+        own_row[pl.ds(0, 1), :] = own_len * own_len
+        own_row[pl.ds(1, 1), :] = own_amp * jnp.sqrt(2.0 * own_len)
+        own_row[pl.ds(2, 1), :] = ((i1 // 32) * 256 + i1 % 32 + yx * 32)[0:1].astype(F32)
 
     def prepare_covar(first, last):
-        i1 = lax.broadcasted_iota(jnp.int32, (1, 512), 1)
-        pos = by_slot((((i1 // 32 + z + 8) % 16) * 256 + i1 % 32).astype(F32))
-
         @pl.loop(first, last)
         def _(t):
-            lrow = len_rel[pl.ds(t, 1), :]
-            arow = amp_rel[pl.ds(t, 1), :]
-            prow = pos + (t * 32).astype(F32)
+            shift = (t * 32).astype(F32)
             for b in range(4):
-                lr = lrow[:, 128 * b : 128 * b + 128]
-                ar = arow[:, 128 * b : 128 * b + 128]
-                pr = prow[:, 128 * b : 128 * b + 128]
+                rows = pl.ds(pl.multiple_of(512 * t + 128 * b, 128), 128)
                 for a in range(4):
-                    inv = lax.rsqrt(len_col[a] + lr)
-                    q = (pos_col[a] - pr) * inv
-                    vals = (amp_col[a] * ar) * (inv * jnp.exp(-(q * q)))
-                    covar[pl.ds(128 * a, 128), pl.ds(pl.multiple_of(512 * t + 128 * b, 128), 128)] = vals.astype(BF16)
+                    part = pl.ds(128 * a, 128)
+                    inv = lax.rsqrt(len_col[t, b] + own_row[pl.ds(0, 1), part])
+                    q = (pos_col[b] - (own_row[pl.ds(2, 1), part] - shift)) * inv
+                    vals = (amp_col[t, b] * own_row[pl.ds(1, 1), part]) * (inv * jnp.exp(-(q * q)))
+                    covar[rows, part] = vals.astype(BF16)
 
     def plane_of(k):
         return (z + k) % 16
@@ -236,7 +235,7 @@
             bounds = send_bounds()
             prepare_rest()
             prepare_rows()
-            prepare_covar(0, 4)
+            prepare_covar(0, 3)
 
         def take(half):
             got = pack_recv[it, pl.ds(8 * half, 8)].astype(F32).reshape(128, 128)
@@ -272,7 +271,7 @@
             send_column(copies, ks, it, 1, mis_send, order_of, mis_recv, slot_of_piece)
         mis_recv[it, slot_of_piece(0)] = mis_send[4]
         if it == 0:
-            prepare_covar(4, 6)
+            prepare_covar(3, 5)
 
         forwards = []
         for part in range(4):
@@ -293,9 +292,9 @@
                 sent.append(c)
             forwards.append(sent)
             if it == 0 and part == 1:
-                prepare_covar(6, 7)
+                prepare_covar(5, 6)
         if it == 0:
-            prepare_covar(7, 8)
+            prepare_covar(6, 8)
 
         smoothed = None
         for parts in ((0, 1), (2,), (3,)):
@@ -307,9 +306,9 @@
                         if m:
                             forwards[part][-m].wait_recv()
                         left.append(gathered[it, t, part])
-                        right.append(covar[:, pl.ds(pl.multiple_of(512 * t + 128 * part, 128), 128)])
-                p = lax.dot_general(
-                    jnp.concatenate(left, axis=1), jnp.concatenate(right, axis=1), NT, preferred_element_type=F32
+                        right.append(covar[pl.ds(pl.multiple_of(512 * t + 128 * part, 128), 128), :])
+                p = jnp.dot(
+                    jnp.concatenate(left, axis=1), jnp.concatenate(right, axis=0), preferred_element_type=F32
                 )
                 smoothed = p if smoothed is None else smoothed + p
         if it == 0:
@@ -383,13 +382,12 @@
             pltpu.VMEM((256, 128), F32),
             pltpu.VMEM((256, 128), F32),
             pltpu.VMEM((256, 1024), BF16),
-            pltpu.VMEM((512, 4096), BF16),
+            pltpu.VMEM((4096, 512), BF16),
             pltpu.VMEM((8, 512), F32),
             pltpu.VMEM((8, 512), F32),
             pltpu.VMEM((8, 512), F32),
-            pltpu.VMEM((8, 512), F32),
-            pltpu.VMEM((4, 128, 128), F32),
-            pltpu.VMEM((4, 128, 128), F32),
+            pltpu.VMEM((8, 4, 128, 128), F32),
+            pltpu.VMEM((8, 4, 128, 128), F32),
             pltpu.VMEM((4, 128, 128), F32),
             pltpu.SemaphoreType.DMA((9,)),
             pltpu.SemaphoreType.REGULAR,

time: 65.4 us -> 64.8 us (level)
  no operation moved by 1% of the time
where the time goes in v4:
time: 64.8 us; the launch traced here: 64.7 us
  Pallas kernels  64 us (99%)
  local copies, waits for them, and re-layouts  0.66 us (1%)
    pallas_call x1, Pallas kernels, per_device(): pl.pallas_call(kernel, out_shape=jax.ShapeDtypeStruct((8, 4096), F32), in...  64 us

profile of v4, /device:TPU:4, one launch (start us, length us, event | category | flops | bytes accessed | tf_op | source)
XLA Modules:
  0.0 64.7 jit_solution(3870801591654704582)
XLA Ops:
  0.0 64.0 %track.1 = f32[8,4096]{1,0:T(8,128)S(1)} custom-call(f32[8,4096]{1,0:T(8,128)} %gains_hbm.1, f32[8]{0:T(128)} %lower_hbm.1, f32[8]{0:T(128)} %upper_hbm.1, bf16[32,1024]{1,0:T(8,128)(2,1)} %response_hbm.1, bf16[32,1024]{1,0:T(8,128)(2,1)} %student_hbm.1, bf16[4,256,256]{2,1,0:T(8,128)(2,1)} %blocks_hbm.1, s32[8,128]{1,0:T(8,128)} %bitcast.5, ...), custom_call_target="tpu_custom_call" | custom-call | tf_op jit(solution)/shard_map/track/pallas_call | solution.py:350
  64.0 0.7 %copy.11 = f32[8,4096]{1,0:T(8,128)} copy(f32[8,4096]{1,0:T(8,128)S(1)} %track.1) | data formatting | bytes 262144

commit v5 on v4

--- a/solution.py
+++ b/solution.py
@@ -104,16 +104,19 @@
         onehot[:, pl.ds(128 * j, 128)] = jnp.where(chan == order[pl.ds(j, 1), :], 1.0, 0.0).astype(BF16)
     loads[2].wait()
 
-    @pl.loop(0, 4)
-    def _(q):
-        rows = pl.ds(pl.multiple_of(q * 256, 256), 256)
-        for b in range(4):
-            spread[:, pl.ds(256 * b, 256)] = jnp.dot(
-                onehot[rows, pl.ds(256 * b, 256)], blocks[b], preferred_element_type=F32
+    def build_matrix(first, last):
+        @pl.loop(first, last)
+        def _(q):
+            rows = pl.ds(pl.multiple_of(q * 256, 256), 256)
+            for b in range(4):
+                spread[:, pl.ds(256 * b, 256)] = jnp.dot(
+                    onehot[rows, pl.ds(256 * b, 256)], blocks[b], preferred_element_type=F32
+                ).astype(BF16)
+            matrix[rows, :] = lax.dot_general(
+                spread[...], onehot[...], NT, preferred_element_type=F32
             ).astype(BF16)
-        matrix[rows, :] = lax.dot_general(
-            spread[...], onehot[...], NT, preferred_element_type=F32
-        ).astype(BF16)
+
+    build_matrix(0, 2)
 
     for c in starts:
         c.wait()
@@ -233,9 +236,10 @@
         pack_recv[it, 4] = pack_send[z]
         if it == 0:
             bounds = send_bounds()
+            build_matrix(2, 4)
             prepare_rest()
             prepare_rows()
-            prepare_covar(0, 3)
+            prepare_covar(0, 1)
 
         def take(half):
             got = pack_recv[it, pl.ds(8 * half, 8)].astype(F32).reshape(128, 128)
@@ -271,7 +275,7 @@
             send_column(copies, ks, it, 1, mis_send, order_of, mis_recv, slot_of_piece)
         mis_recv[it, slot_of_piece(0)] = mis_send[4]
         if it == 0:
-            prepare_covar(3, 5)
+            prepare_covar(1, 3)
 
         forwards = []
         for part in range(4):
@@ -292,9 +296,9 @@
                 sent.append(c)
             forwards.append(sent)
             if it == 0 and part == 1:
-                prepare_covar(5, 6)
+                prepare_covar(3, 5)
         if it == 0:
-            prepare_covar(6, 8)
+            prepare_covar(5, 8)
 
         smoothed = None
         for parts in ((0, 1), (2,), (3,)):

time: 64.8 us -> 64 us (0.988)
  Pallas kernels: 64 us -> 63.2 us
    pallas_call x1, Pallas kernels: 64 us -> 63.2 us  [per_device(): pl.pallas_call(kernel, out_shape=jax.ShapeDtypeStruct((8, 4096), F32), in...]
where the time goes in v5:
time: 64 us; the launch traced here: 63.9 us
  Pallas kernels  63.2 us (99%)
  local copies, waits for them, and re-layouts  0.66 us (1%)
    pallas_call x1, Pallas kernels, per_device(): pl.pallas_call(kernel, out_shape=jax.ShapeDtypeStruct((8, 4096), F32), in...  63.2 us

profile of v5, /device:TPU:4, one launch (start us, length us, event | category | flops | bytes accessed | tf_op | source)
XLA Modules:
  0.0 63.9 jit_solution(729754321753030923)
XLA Ops:
  0.0 63.2 %track.1 = f32[8,4096]{1,0:T(8,128)S(1)} custom-call(f32[8,4096]{1,0:T(8,128)} %gains_hbm.1, f32[8]{0:T(128)} %lower_hbm.1, f32[8]{0:T(128)} %upper_hbm.1, bf16[32,1024]{1,0:T(8,128)(2,1)} %response_hbm.1, bf16[32,1024]{1,0:T(8,128)(2,1)} %student_hbm.1, bf16[4,256,256]{2,1,0:T(8,128)(2,1)} %blocks_hbm.1, s32[8,128]{1,0:T(8,128)} %bitcast.5, ...), custom_call_target="tpu_custom_call" | custom-call | tf_op jit(solution)/shard_map/track/pallas_call | solution.py:354
  63.2 0.7 %copy.11 = f32[8,4096]{1,0:T(8,128)} copy(f32[8,4096]{1,0:T(8,128)S(1)} %track.1) | data formatting | bytes 262144

commit v6 on v5

--- a/solution.py
+++ b/solution.py
@@ -225,6 +225,7 @@
     def slot_of_piece(k):
         return FROM.index((8 - k) % 16 - 8)
 
+    pending = []
     for it in range(ITERS):
         now = start_recv[...].reshape(64, 512) if it == 0 else state[...]
         for a in range(4):
@@ -234,6 +235,8 @@
         copies = {}
         send_column(copies, FAR + CLOSE, it, 0, pack_send, plane_of, pack_recv, order_from)
         pack_recv[it, 4] = pack_send[z]
+        for c in pending:
+            c.wait_send()
         if it == 0:
             bounds = send_bounds()
             build_matrix(2, 4)
@@ -327,11 +330,7 @@
             state[...] = nxt
         else:
             final_send[...] = nxt.reshape(8, 8, 512)
-        for c in copies.values():
-            c.wait_send()
-        for sent in forwards:
-            for c in sent:
-                c.wait_send()
+        pending = list(copies.values()) + [c for sent in forwards for c in sent]
 
     copies = []
     for k in PLANE:
@@ -340,6 +339,8 @@
         c.start()
         copies.append(c)
     final_recv[yx] = final_send[yx]
+    for c in pending:
+        c.wait_send()
     for c in copies:
         c.wait()
     for h in range(2):

time: 64 us -> 63.9 us (level)
  no operation moved by 1% of the time
where the time goes in v6:
time: 63.9 us; the launch traced here: 63.7 us
  Pallas kernels  63.1 us (99%)
  local copies, waits for them, and re-layouts  0.66 us (1%)
    pallas_call x1, Pallas kernels, per_device(): pl.pallas_call(kernel, out_shape=jax.ShapeDtypeStruct((8, 4096), F32), in...  63.1 us

profile of v6, /device:TPU:4, one launch (start us, length us, event | category | flops | bytes accessed | tf_op | source)
XLA Modules:
  0.0 63.7 jit_solution(17807237996612876683)
XLA Ops:
  0.0 63.1 %track.1 = f32[8,4096]{1,0:T(8,128)S(1)} custom-call(f32[8,4096]{1,0:T(8,128)} %gains_hbm.1, f32[8]{0:T(128)} %lower_hbm.1, f32[8]{0:T(128)} %upper_hbm.1, bf16[32,1024]{1,0:T(8,128)(2,1)} %response_hbm.1, bf16[32,1024]{1,0:T(8,128)(2,1)} %student_hbm.1, bf16[4,256,256]{2,1,0:T(8,128)(2,1)} %blocks_hbm.1, s32[8,128]{1,0:T(8,128)} %bitcast.5, ...), custom_call_target="tpu_custom_call" | custom-call | tf_op jit(solution)/shard_map/track/pallas_call | solution.py:355
  63.1 0.7 %copy.11 = f32[8,4096]{1,0:T(8,128)} copy(f32[8,4096]{1,0:T(8,128)S(1)} %track.1) | data formatting | bytes 262144
